TPU v7x, 512 devices: a whole 4x4x16 slice. The times are simulated.
512 devices in a mesh: narrow: 16 (over z), wide: 32 (over y, x, core).
Axes of the slice: x: 4, y: 4, z: 16, core: 2. Of those that a mesh axis runs over, the one named last changes fastest.
Arguments:
- sources: float32 [16, 64, 128, 256], P(None, 'wide', 'narrow')
- well_columns: int32 [16], replicated, may hold values from 0 to 8191
- column_active: int32 [64, 128], P('wide', 'narrow'), may hold values 0 or 1
- perm_root: float32 [64, 128, 256], P('wide', 'narrow'), may hold values from 0.5 to 2
- storage_term: float32 [64, 128, 256], P('wide', 'narrow'), may hold values from 0.2 to 2
- inverse_blocks: bfloat16 [64, 128, 2, 128, 128], P('wide', 'narrow')
Outputs:
- solution: float32 [16, 64, 128, 256], P(None, 'wide', 'narrow')
- residual: float32 [16, 64, 128, 256], P(None, 'wide', 'narrow')
All inputs are finite; a program needn't handle non-finite values. No bound on the sum of `column_active` on one device may be relied on, other than what follows from the above.
Results may differ from a plain program's by a relative error of at most 0.0085.
Values sent between devices are 32-bit elements; how exact they have to be, the bound alone decides.
A program may use at most 64 MiB of HBM per device.

v0:
```python
import jax
import jax.numpy as jnp
from jax import lax
from jax.sharding import PartitionSpec as P

ITERS = 3


WELL_RATE = 4.0


def with_halo(x, sides, width):
    for axis, dim in sides:
        peers, length = (lax.axis_size(axis), x.shape[dim])
        up = [(i, (i + 1) % peers) for i in range(peers - 1)]
        down = [(j, i) for i, j in up]
        last = lax.slice_in_dim(x, length - width, length, axis=dim)
        first = lax.slice_in_dim(x, 0, width, axis=dim)
        before = lax.ppermute(last, axis, up)
        after = lax.ppermute(first, axis, down)
        x = jnp.concatenate([before, x, after], axis=dim)
    return x


def coupling(padded, coef_pad):
    center = padded[:, 1:-1, 1:-1]
    coef = coef_pad[1:-1, 1:-1]
    total = coef_pad[2:, 1:-1] * (center - padded[:, 2:, 1:-1]) + coef_pad[:-2, 1:-1] * (
        center - padded[:, :-2, 1:-1]
    )
    total = (
        total
        + coef_pad[1:-1, 2:] * (center - padded[:, 1:-1, 2:])
        + coef_pad[1:-1, :-2] * (center - padded[:, 1:-1, :-2])
    )
    zero_layer = jnp.zeros_like(center[..., :1])
    zero_coef = jnp.zeros_like(coef[..., :1])
    upper = jnp.concatenate([center[..., 1:], zero_layer], -1)
    upper_coef = jnp.concatenate([coef[..., 1:], zero_coef], -1)
    lower = jnp.concatenate([zero_layer, center[..., :-1]], -1)
    lower_coef = jnp.concatenate([zero_coef, coef[..., :-1]], -1)
    total = total + upper_coef * (center - upper) + lower_coef * (center - lower)
    return coef * total


def operate(values, diag_term, coef, coef_pad):
    if coef_pad is None:
        stacked = jnp.concatenate([values, coef[None]], 0)
    else:
        stacked = values
    padded = with_halo(stacked, (("narrow", 2), ("wide", 1)), 1)
    if coef_pad is None:
        coef_pad = padded[-1]
        padded = padded[:-1]
    return (diag_term * values + coupling(padded, coef_pad), coef_pad)


def precondition(values, inverse_blocks):
    count, cols_x, cols_y, layers = values.shape
    blocks = inverse_blocks.shape[2]
    shaped = values.astype(jnp.bfloat16).reshape(count, cols_x, cols_y, blocks, layers // blocks)
    output = jnp.einsum(
        "xybij,kxybj->kxybi", inverse_blocks, shaped, preferred_element_type=jnp.float32
    )
    return output.reshape(count, cols_x, cols_y, layers)


def local_gram(left, right):
    return jnp.einsum("kxyz,lxyz->kl", left, right, precision=lax.Precision.HIGHEST)


def combine(values, coefs):
    return jnp.einsum("kxyz,kl->lxyz", values, coefs, precision=lax.Precision.HIGHEST)


def solve_gram(matrix, target):
    sym = 0.5 * (matrix + matrix.T)
    factor = jnp.linalg.cholesky(sym)
    inner = lax.linalg.triangular_solve(factor, target, left_side=True, lower=True)
    return lax.linalg.triangular_solve(factor, inner, left_side=True, lower=True, transpose_a=True)


def residual_sum(left, right):
    return lax.psum(local_gram(left, right), ("narrow", "wide"))


def curvature_sum(left, right):
    return lax.psum(local_gram(left, right), ("narrow", "wide"))


def on_device(sources, well_columns, column_active, perm_root, storage_term, inverse_blocks):
    cols_x, cols_y = column_active.shape
    grid_y = cols_y * lax.axis_size("narrow")
    first_x = lax.axis_index("wide") * cols_x
    first_y = lax.axis_index("narrow") * cols_y
    column_ids = (
        (first_x + jnp.arange(cols_x, dtype=jnp.int32))[:, None] * grid_y
        + first_y
        + jnp.arange(cols_y, dtype=jnp.int32)[None, :]
    )
    wells = (column_ids[None] == well_columns[:, None, None]).astype(jnp.float32)
    active = column_active.astype(jnp.float32)[..., None]
    coef = perm_root * active
    diag_term = active * storage_term + (1.0 - active)
    residual = sources + WELL_RATE * wells[..., None]
    solution = jnp.zeros_like(residual)
    zset = precondition(residual, inverse_blocks)
    coef_pad = None
    res_gram = residual_sum(zset, residual)
    direction = zset
    for iteration in range(ITERS):
        image, coef_pad = operate(direction, diag_term, coef, coef_pad)
        curv_gram = curvature_sum(direction, image)
        step_size = solve_gram(curv_gram, res_gram)
        solution = solution + combine(direction, step_size)
        residual = residual - combine(image, step_size)
        if iteration + 1 < ITERS:
            zset = precondition(residual, inverse_blocks)
            new_gram = residual_sum(zset, residual)
            conj_coef = solve_gram(res_gram, new_gram)
            direction = zset + combine(direction, conj_coef)
            res_gram = new_gram
    return (solution, residual)


def solution(mesh):
    in_specs = (
        P(None, "wide", "narrow", None),
        P(),
        P("wide", "narrow"),
        P("wide", "narrow", None),
        P("wide", "narrow", None),
        P("wide", "narrow", None, None, None),
    )
    out_specs = (P(None, "wide", "narrow", None), P(None, "wide", "narrow", None))
    return jax.shard_map(
        on_device, mesh=mesh, in_specs=in_specs, out_specs=out_specs, check_vma=False
    )
```

profile of v0, /device:TPU:1, one launch (start us, length us, event | category | flops | bytes accessed | tf_op | source)
XLA Modules:
  0.0 604.0 jit_solution(7045459315750668547)
XLA Ops:
  3.0 1.6 convolution_bitcast_fusion.2
  5.1 1.3 collective-permute-start.1
  6.4 5.0 collective-permute-start
  12.6 8.9 %collective-permute-start.3 = (f32[17,1,10,256]{3,0,2,1:T(8,128)S(1)}, f32[17,1,10,256]{3,0,2,1:T(8,128)S(1)}, u32[]{:S(2)}, u32[]{:S(2)}) collective-permute-start(f32[17,1,10,256]{3,0,2,1:T(8,128)S(1)} %get-tuple-element.11), channel_id=1, source_target_pairs={{1,0},{2,1},{3,2},{4,3},{5,4},{6,5},{7,6},{8,7},{9,8},{10,9},{11,1... | collective-permute-start | bytes 522248 | tf_op jit(solution)/shard_map/ppermute | solution.py:20
  21.5 1.9 collective-permute-start.2
  27.7 109.5 %all-reduce.8 = (f32[16,16]{1,0:T(8,128)S(1)}, f32[16,16]{1,0:T(8,128)S(1)}) all-reduce(f32[16,16]{1,0:T(8,128)S(1)} %convolution_bitcast_fusion.12, f32[16,16]{1,0:T(8,128)S(1)} %convolution_bitcast_fusion.13), channel_id=1, replica_groups=mesh['narrow'=16,'wide'=32] {'narrow','wide'}, use_global_device_ids=true, to_apply=%region_3.0 | all-reduce | flops 512 | bytes 4096 | tf_op jit(solution)/shard_map/psum | solution.py:84
  137.5 1.5 cholesky.100
  140.3 1.2 custom-call.19
  141.6 1.5 cholesky.89
  147.8 100.5 %psum.44 = f32[16,16]{1,0:T(8,128)S(1)} all-reduce(f32[16,16]{1,0:T(8,128)S(1)} %convolution_bitcast_fusion.11), channel_id=1, replica_groups=mesh['narrow'=16,'wide'=32] {'narrow','wide'}, use_global_device_ids=true, to_apply=%region_4.8 | all-reduce | flops 256 | bytes 2048 | tf_op jit(solution)/shard_map/psum | solution.py:84
  249.6 1.5 cholesky.122
  251.7 1.3 collective-permute-start.5
  253.0 4.0 collective-permute-start.4
  259.0 3.1 collective-permute-start.6
  262.1 2.4 collective-permute-start.7
  267.5 103.6 %psum.45 = f32[16,16]{1,0:T(8,128)S(1)} all-reduce(f32[16,16]{1,0:T(8,128)S(1)} %convolution_bitcast_fusion.10), channel_id=1, replica_groups=mesh['narrow'=16,'wide'=32] {'narrow','wide'}, use_global_device_ids=true, to_apply=%region_5.9 | all-reduce | flops 256 | bytes 2048 | tf_op jit(solution)/shard_map/psum | solution.py:88
  371.3 1.5 cholesky.111
  377.2 100.1 %psum.46 = f32[16,16]{1,0:T(8,128)S(1)} all-reduce(f32[16,16]{1,0:T(8,128)S(1)} %convolution_bitcast_fusion.9), channel_id=1, replica_groups=mesh['narrow'=16,'wide'=32] {'narrow','wide'}, use_global_device_ids=true, to_apply=%region_6.10 | all-reduce | flops 256 | bytes 2048 | tf_op jit(solution)/shard_map/psum | solution.py:84
  478.1 1.3 collective-permute-start.9
  479.4 4.0 collective-permute-start.8
  484.4 3.7 collective-permute-start.10
  488.2 2.1 collective-permute-start.11
  493.2 103.8 %psum.47 = f32[16,16]{1,0:T(8,128)S(1)} all-reduce(f32[16,16]{1,0:T(8,128)S(1)} %convolution_bitcast_fusion.8), channel_id=1, replica_groups=mesh['narrow'=16,'wide'=32] {'narrow','wide'}, use_global_device_ids=true, to_apply=%region_7.11 | all-reduce | flops 256 | bytes 2048 | tf_op jit(solution)/shard_map/psum | solution.py:88
  597.2 1.5 cholesky.133
  (129 shorter events, 36.2 us)
Async XLA Ops:
  0.6 2.4 copy-start
  0.6 0.8 copy-start.3
  0.7 0.8 copy-start.2
  2.3 0.7 copy-start.4
  5.1 6.3 %collective-permute-start.1 = (f32[17,2,1,256]{3,0,2,1:T(8,128)S(1)}, f32[17,2,1,256]{3,0,2,1:T(8,128)S(1)}, u32[]{:S(2)}, u32[]{:S(2)}) collective-permute-start(f32[17,2,1,256]{3,0,2,1:T(8,128)S(1)} %get-tuple-element.13), channel_id=1, source_target_pairs={{32,0},{64,32},{96,64},{128,96},{160,128},{192,160},{224,192},{256... | collective-permute-start | bytes 104456 | tf_op jit(solution)/shard_map/ppermute | solution.py:20
  6.4 6.2 %collective-permute-start = (f32[17,2,1,256]{3,0,2,1:T(8,128)S(1)}, f32[17,2,1,256]{3,0,2,1:T(8,128)S(1)}, u32[]{:S(2)}, u32[]{:S(2)}) collective-permute-start(f32[17,2,1,256]{3,0,2,1:T(8,128)S(1)} %get-tuple-element.14), channel_id=1, source_target_pairs={{0,32},{32,64},{64,96},{96,128},{128,160},{160,192},{192,224},{224... | collective-permute-start | bytes 104456 | tf_op jit(solution)/shard_map/ppermute | solution.py:19
  12.6 12.8 %collective-permute-start.3 = (f32[17,1,10,256]{3,0,2,1:T(8,128)S(1)}, f32[17,1,10,256]{3,0,2,1:T(8,128)S(1)}, u32[]{:S(2)}, u32[]{:S(2)}) collective-permute-start(f32[17,1,10,256]{3,0,2,1:T(8,128)S(1)} %get-tuple-element.11), channel_id=1, source_target_pairs={{1,0},{2,1},{3,2},{4,3},{5,4},{6,5},{7,6},{8,7},{9,8},{10,9},{11,1... | collective-permute-start | bytes 522248 | tf_op jit(solution)/shard_map/ppermute | solution.py:20
  21.5 5.0 collective-permute-start.2
  23.8 1.0 copy-start.1
  251.7 7.2 %collective-permute-start.5 = (f32[16,2,1,256]{3,0,2,1:T(8,128)S(1)}, f32[16,2,1,256]{3,0,2,1:T(8,128)S(1)}, u32[]{:S(2)}, u32[]{:S(2)}) collective-permute-start(f32[16,2,1,256]{3,0,2,1:T(8,128)S(1)} %get-tuple-element.25), channel_id=1, source_target_pairs={{32,0},{64,32},{96,64},{128,96},{160,128},{192,160},{224,192},{256... | collective-permute-start | bytes 98312 | tf_op jit(solution)/shard_map/ppermute | solution.py:20
  253.0 5.9 collective-permute-start.4
  259.0 6.6 %collective-permute-start.6 = (f32[16,1,10,256]{3,0,2,1:T(8,128)S(1)}, f32[16,1,10,256]{3,0,2,1:T(8,128)S(1)}, u32[]{:S(2)}, u32[]{:S(2)}) collective-permute-start(f32[16,1,10,256]{3,0,2,1:T(8,128)S(1)} %get-tuple-element.17), channel_id=1, source_target_pairs={{1,0},{2,1},{3,2},{4,3},{5,4},{6,5},{7,6},{8,7},{9,8},{10,9},{11,1... | collective-permute-start | bytes 491528 | tf_op jit(solution)/shard_map/ppermute | solution.py:20
  262.1 4.7 collective-permute-start.7
  478.1 5.7 collective-permute-start.9
  479.4 5.0 collective-permute-start.8
  484.4 6.9 %collective-permute-start.10 = (f32[16,1,10,256]{3,0,2,1:T(8,128)S(1)}, f32[16,1,10,256]{3,0,2,1:T(8,128)S(1)}, u32[]{:S(2)}, u32[]{:S(2)}) collective-permute-start(f32[16,1,10,256]{3,0,2,1:T(8,128)S(1)} %get-tuple-element.15), channel_id=1, source_target_pairs={{1,0},{2,1},{3,2},{4,3},{5,4},{6,5},{7,6},{8,7},{9,8},{10,9},{11,1... | collective-permute-start | bytes 491528 | tf_op jit(solution)/shard_map/ppermute | solution.py:20
  488.2 4.4 collective-permute-start.11
where the time goes:
time: 605 us; the launch traced here: 604 us
  blocking collectives  517 us (85%)
  starting transfers between devices  39.1 us (6%)
  other arithmetic  22 us (4%)
  matrix products  11.4 us (2%)
  waiting for transfers between devices  6.8 us (1%)
  local copies, waits for them, and re-layouts  6.24 us (1%)
    psum x3, blocking collectives, residual_sum(): return lax.psum(local_gram(left, right), ('narrow', 'wide'))  310 us
    psum x2, blocking collectives, curvature_sum(): return lax.psum(local_gram(left, right), ('narrow', 'wide'))  207 us
    ppermute x6, starting transfers between devices, with_halo(): after = lax.ppermute(first, axis, down)  19.6 us
    ppermute x6, starting transfers between devices, with_halo(): before = lax.ppermute(last, axis, up)  19.5 us
  transfers between devices with their start and end apart: 12, of which 7 were waited for; matrix products, arithmetic and copies ran while one was open for 1% of the time, Pallas kernels for 0%

commit v1 on v0

v1 whole, which is shorter than its diff:
```python
import functools

import jax
import jax.numpy as jnp
from jax import lax
from jax.experimental import pallas as pl
from jax.experimental.pallas import tpu as pltpu
from jax.sharding import PartitionSpec as P

BASIS = 3
WELL_RATE = 4.0
BASIS_SCALE = 1.0 / 16.0
MESH = pl.DeviceIdType.MESH
EXACT = lax.Precision.HIGHEST
F32 = jnp.float32


def dot_nt(left, right):
    return lax.dot_general(left, right, (((1,), (1,)), ((), ())), precision=EXACT, preferred_element_type=F32)


def dot_nn(left, right):
    return lax.dot_general(left, right, (((1,), (0,)), ((), ())), precision=EXACT, preferred_element_type=F32)


def kernel(
    n_wide,
    n_narrow,
    src_hbm,
    wells_hbm,
    active_hbm,
    perm_hbm,
    storage_hbm,
    inv_hbm,
    sol_ref,
    res_ref,
    rhs,
    wells,
    active,
    perm,
    storage,
    inv,
    coef,
    coef_y,
    coef_x,
    coef_pad,
    diag,
    zs,
    ws,
    halo_x,
    halo_y,
    part,
    rows_in,
    plane_in,
    plane,
    all_rows,
    total,
    load_sem,
    coef_send,
    coef_recv,
    halo_send,
    halo_recv,
    sum_send,
    sum_recv,
):
    kk, cx, cy, nz = src_hbm.shape
    blk = inv_hbm.shape[-1]
    nb = inv_hbm.shape[2]
    me_w, me_n = lax.axis_index("wide"), lax.axis_index("narrow")
    right, left = lax.rem(me_w + 1, n_wide), lax.rem(me_w + n_wide - 1, n_wide)
    above, below = lax.rem(me_n + 1, n_narrow), lax.rem(me_n + n_narrow - 1, n_narrow)

    barrier = pltpu.get_barrier_semaphore()

    @pl.loop(1, n_narrow)
    def _(d):
        peer = lax.rem(me_n + d, n_narrow)
        pl.semaphore_signal(barrier, inc=1, device_id={"narrow": peer}, device_id_type=MESH)

    @pl.loop(1, n_wide)
    def _(d):
        peer = lax.rem(me_w + d, n_wide)
        pl.semaphore_signal(barrier, inc=1, device_id={"wide": peer}, device_id_type=MESH)

    loads = [
        pltpu.make_async_copy(wells_hbm, wells, load_sem.at[0]),
        pltpu.make_async_copy(active_hbm, active, load_sem.at[1]),
        pltpu.make_async_copy(perm_hbm, perm, load_sem.at[2]),
        pltpu.make_async_copy(storage_hbm, storage, load_sem.at[3]),
        pltpu.make_async_copy(inv_hbm, inv, load_sem.at[4]),
    ]
    columns = [(x, y) for x in range(cx) for y in range(cy)]
    for at, (x, y) in enumerate(columns):
        loads.append(pltpu.make_async_copy(src_hbm.at[:, x, y, :], rhs.at[x, y], load_sem.at[5 + at]))
    for load in loads:
        load.start()
    for load in loads[:4]:
        load.wait()

    row = lax.broadcasted_iota(jnp.int32, (cy, nz), 0)
    for x in range(cx):
        on = jnp.zeros((cy, nz), F32)
        for y in range(cy):
            on = jnp.where(row == y, active[x, y].astype(F32), on)
        coef[x] = perm[x] * on
        diag[x] = on * storage[x] + (1.0 - on)

    ids = lax.broadcasted_iota(jnp.int32, (kk, nz), 0)
    well_of = jnp.zeros((kk, nz), jnp.int32)
    for k in range(kk):
        well_of = jnp.where(ids == k, wells[k], well_of)
    for load in loads[4:]:
        load.wait()

    def precondition(get, put):
        for x, y in columns:
            value = get(x, y)
            high = value.astype(jnp.bfloat16)
            low = (value - high.astype(F32)).astype(jnp.bfloat16)
            both = jnp.concatenate([high, low], axis=0)
            for b in range(nb):
                out = lax.dot_general(
                    both[:, b * blk : (b + 1) * blk],
                    inv[x, y, b],
                    (((1,), (0,)), ((), ())),
                    preferred_element_type=F32,
                )
                put(x, y, b, out[:kk] + out[kk:])

    first_x, first_y = me_w * cx, me_n * cy
    for x, y in columns:
        here = (first_x + x) * (n_narrow * cy) + first_y + y
        rhs[x, y] = rhs[x, y] + jnp.where(well_of == here, WELL_RATE, 0.0)

    def store_z(i, scale):
        def put(x, y, b, value):
            zs[i, x, y, :, b * blk : (b + 1) * blk] = value * scale if scale != 1.0 else value

        return put

    precondition(lambda x, y: rhs[x, y], store_z(0, 1.0))

    pl.semaphore_wait(barrier, n_narrow + n_wide - 2)

    def remote(source, target, send, recv, device):
        return pltpu.make_async_remote_copy(
            src_ref=source, dst_ref=target, send_sem=send, recv_sem=recv, device_id=device, device_id_type=MESH
        )

    def send_halo(i):
        copies = [
            remote(zs.at[i, cx - 1], halo_x.at[i, 0], halo_send.at[i, 0], halo_recv.at[i, 0], {"wide": right}),
            remote(zs.at[i, 0], halo_x.at[i, 1], halo_send.at[i, 1], halo_recv.at[i, 1], {"wide": left}),
            remote(zs.at[i, :, cy - 1], halo_y.at[i, 0], halo_send.at[i, 2], halo_recv.at[i, 2], {"narrow": above}),
            remote(zs.at[i, :, 0], halo_y.at[i, 1], halo_send.at[i, 3], halo_recv.at[i, 3], {"narrow": below}),
        ]
        for copy in copies:
            copy.start()
        return copies

    coef_copies = [
        remote(coef.at[cx - 1], coef_x.at[0], coef_send.at[0], coef_recv.at[0], {"wide": right}),
        remote(coef.at[0], coef_x.at[1], coef_send.at[1], coef_recv.at[1], {"wide": left}),
        remote(coef, coef_y.at[0], coef_send.at[2], coef_recv.at[2], {"narrow": above}),
        remote(coef, coef_y.at[1], coef_send.at[3], coef_recv.at[3], {"narrow": below}),
    ]
    for copy in coef_copies:
        copy.start()
    flying = send_halo(0)

    has_left = jnp.where(me_w == 0, 0.0, 1.0)
    has_right = jnp.where(me_w == n_wide - 1, 0.0, 1.0)
    has_below = jnp.where(me_n == 0, 0.0, 1.0)
    has_above = jnp.where(me_n == n_narrow - 1, 0.0, 1.0)

    def spread(line):
        return jnp.broadcast_to(line, (8, nz))

    for x, y in columns:
        coef_pad[x + 1, y + 1] = spread(coef[x, y : y + 1])
    for copy in coef_copies:
        copy.wait()
    for y in range(cy):
        coef_pad[0, y + 1] = spread(coef_x[0, y : y + 1] * has_left)
        coef_pad[cx + 1, y + 1] = spread(coef_x[1, y : y + 1] * has_right)
    for x in range(cx):
        coef_pad[x + 1, 0] = spread(coef_y[0, x, cy - 1 : cy] * has_below)
        coef_pad[x + 1, cy + 1] = spread(coef_y[1, x, 0:1] * has_above)

    lane8 = lax.broadcasted_iota(jnp.int32, (8, nz), 1)

    def next_layer(value):
        return jnp.where(lane8 == nz - 1, 0.0, pltpu.roll(value, nz - 1, 1))

    def last_layer(value):
        return jnp.where(lane8 == 0, 0.0, pltpu.roll(value, 1, 1))

    dfull = total

    def build_diag():
        for x, y in columns:
            c = coef_pad[x + 1, y + 1]
            around = coef_pad[x, y + 1] + coef_pad[x + 2, y + 1] + coef_pad[x + 1, y] + coef_pad[x + 1, y + 2]
            around += next_layer(c) + last_layer(c)
            dfull[x, y] = spread(diag[x, y : y + 1]) + c * around

    build_diag()

    def operate(i):
        for x, y in columns:
            c = coef_pad[x + 1, y + 1]
            west, east = coef_pad[x, y + 1], coef_pad[x + 2, y + 1]
            south, north = coef_pad[x + 1, y], coef_pad[x + 1, y + 2]
            for h in range(kk // 8):
                ks = pl.ds(8 * h, 8)
                v = zs[i, x, y, ks]
                u = c * v
                near = next_layer(u) + last_layer(u)
                near += west * (zs[i, x - 1, y, ks] if x > 0 else halo_x[i, 0, y, ks])
                near += east * (zs[i, x + 1, y, ks] if x < cx - 1 else halo_x[i, 1, y, ks])
                near += south * (zs[i, x, y - 1, ks] if y > 0 else halo_y[i, 0, x, ks])
                near += north * (zs[i, x, y + 1, ks] if y < cy - 1 else halo_y[i, 1, x, ks])
                ws[i, x, y, ks] = dfull[x, y] * v - c * near

    def gram(lefts, rights):
        acc = None
        for x, y in columns:
            left_rows = jnp.concatenate([ref[x, y] for ref in lefts], axis=0)
            right_rows = jnp.concatenate([ref[x, y] for ref in rights], axis=0)
            product = dot_nt(left_rows, right_rows)
            acc = product if acc is None else acc + product
        return acc

    z_refs = [zs.at[i] for i in range(BASIS)]
    w_refs = [ws.at[i] for i in range(BASIS)]

    blocks = {}
    for i in range(BASIS):
        if i > 0:
            precondition(lambda x, y: ws[i - 1, x, y], store_z(i, BASIS_SCALE))
            flying = send_halo(i)
        known = gram([rhs] + w_refs[:i], [z_refs[i]])
        for r in range(i + 1):
            blocks[r, i] = known[kk * r : kk * (r + 1)]
        if i > 0:
            mirror = gram([z_refs[i]], w_refs[:i])
            for r in range(i):
                blocks[i + 1, r] = mirror[:, kk * r : kk * (r + 1)]
        for copy in flying:
            copy.wait()
        operate(i)
        own = gram([w_refs[i]], [z_refs[i]])
        blocks[i + 1, i] = own
    half = (BASIS + 1) * kk // 2
    span = BASIS * kk
    pad = jnp.zeros((half, 64 - span), F32)
    sums = jnp.concatenate(
        [jnp.concatenate([blocks[r, i] for r in range(BASIS + 1)], axis=0) for i in range(BASIS)], axis=1
    )
    sums = jnp.concatenate([sums[:half], pad, sums[half:], pad], axis=1)
    for r in range(half):
        part[r] = sums[r : r + 1]

    def start_all(axis, me, count, source, target, stage):
        @pl.loop(1, count)
        def _(d):
            peer = lax.rem(me + d, count)
            remote(source(peer), target(d), sum_send.at[stage], sum_recv.at[stage], {axis: peer}).start()

    def wait_all(buffer, count, stage, axis, peer):
        whole = buffer.at[pl.ds(0, count - 1)]
        done = remote(whole, whole, sum_send.at[stage], sum_recv.at[stage], {axis: peer})
        done.wait_send()
        done.wait_recv()

    start_all("wide", me_w, n_wide, lambda peer: part.at[peer], lambda d: rows_in.at[d - 1], 0)
    mine = part[me_w]
    wait_all(rows_in, n_wide, 0, "wide", right)
    for d in range(n_wide - 1):
        mine = mine + rows_in[d]
    plane[...] = mine
    start_all("narrow", me_n, n_narrow, lambda peer: plane, lambda d: plane_in.at[d - 1], 1)
    wait_all(plane_in, n_narrow, 1, "narrow", above)
    for d in range(n_narrow - 1):
        mine = mine + plane_in[d]
    all_rows[me_w] = mine
    start_all("wide", me_w, n_wide, lambda peer: all_rows.at[me_w], lambda d: all_rows.at[me_w], 2)
    wait_all(all_rows, n_wide, 2, "wide", right)

    packed = jnp.concatenate([all_rows[r] for r in range(half)], axis=0)
    low = packed
    high = pltpu.roll(packed, 64, 1)
    system = jnp.concatenate([low, high], axis=0)
    lanes = lax.broadcasted_iota(jnp.int32, (1, 128), 1)
    for k in range(span):
        pivot_row = system[kk + k : kk + k + 1]
        column = system[:, k : k + 1]
        factor = pivot_row / pivot_row[:, k : k + 1]
        inverse = 1.0 / pivot_row[:, k : k + 1]
        system = jnp.where(lanes == k, column * inverse, system - column * factor)
    y = system[:kk, :span]

    for x, yy in columns:
        basis = jnp.concatenate([zs[i, x, yy] for i in range(BASIS)], axis=0)
        image = jnp.concatenate([ws[i, x, yy] for i in range(BASIS)], axis=0)
        sol_ref[x, yy] = dot_nn(y, basis)
        res_ref[x, yy] = rhs[x, yy] - dot_nn(y, image)


def solution(mesh):
    n_wide, n_narrow = mesh.shape["wide"], mesh.shape["narrow"]

    def on_device(sources, well_columns, column_active, perm_root, storage_term, inverse_blocks):
        kk, cx, cy, nz = sources.shape
        nb, blk = inverse_blocks.shape[2], inverse_blocks.shape[3]
        rows = (BASIS + 1) * kk // 2
        field = jax.ShapeDtypeStruct((cx, cy, kk, nz), F32)
        dma = pltpu.SemaphoreType.DMA
        vmem = pltpu.VMEM
        out = pl.pallas_call(
            functools.partial(kernel, n_wide, n_narrow),
            out_shape=(field, field),
            in_specs=[pl.BlockSpec(memory_space=pl.ANY)] * 6,
            out_specs=(pl.BlockSpec(memory_space=vmem),) * 2,
            scratch_shapes=[
                vmem((cx, cy, kk, nz), F32),
                pltpu.SMEM(well_columns.shape, jnp.int32),
                pltpu.SMEM(column_active.shape, jnp.int32),
                vmem((cx, cy, nz), F32),
                vmem((cx, cy, nz), F32),
                vmem(inverse_blocks.shape, inverse_blocks.dtype),
                vmem((cx, cy, nz), F32),
                vmem((2, cx, cy, nz), F32),
                vmem((2, cy, nz), F32),
                vmem((cx + 2, cy + 2, 8, nz), F32),
                vmem((cx, cy, nz), F32),
                vmem((BASIS, cx, cy, kk, nz), F32),
                vmem((BASIS, cx, cy, kk, nz), F32),
                vmem((BASIS, 2, cy, kk, nz), F32),
                vmem((BASIS, 2, cx, kk, nz), F32),
                vmem((rows, 1, 128), F32),
                vmem((n_wide - 1, 1, 128), F32),
                vmem((n_narrow - 1, 1, 128), F32),
                vmem((1, 128), F32),
                vmem((rows, 1, 128), F32),
                vmem((cx, cy, 8, nz), F32),
                dma((5 + cx * cy,)),
                dma((4,)),
                dma((4,)),
                dma((BASIS, 4)),
                dma((BASIS, 4)),
                dma((3,)),
                dma((3,)),
            ],
            compiler_params=pltpu.CompilerParams(collective_id=0, has_side_effects=True),
        )(sources, well_columns, column_active, perm_root, storage_term, inverse_blocks)
        return tuple(jnp.transpose(value, (2, 0, 1, 3)) for value in out)

    in_specs = (
        P(None, "wide", "narrow", None),
        P(),
        P("wide", "narrow"),
        P("wide", "narrow", None),
        P("wide", "narrow", None),
        P("wide", "narrow", None, None, None),
    )
    out_specs = (P(None, "wide", "narrow", None), P(None, "wide", "narrow", None))
    return jax.shard_map(
        on_device, mesh=mesh, in_specs=in_specs, out_specs=out_specs, check_vma=False
    )
```

time: 605 us -> 60.7 us (0.10)
  blocking collectives: 517 us -> 0 us
  Pallas kernels: 0 us -> 57.2 us
  starting transfers between devices: 39.1 us -> 0 us
  other arithmetic: 22 us -> 0 us
  matrix products: 11.4 us -> 0 us
  waiting for transfers between devices: 6.8 us -> 0 us
    psum x5 -> x0, blocking collectives: 517 us -> none  [the longest x3 310 us: residual_sum(): return lax.psum(local_gram(left, right), ('narrow', 'wide'))]
    pallas_call x0 -> x1, Pallas kernels: none -> 57.2 us  [on_device(): pl.pallas_call(functools.partial(kernel, n_wide, n_narrow), out_shape=(fi...]
    ppermute x12 -> x0, starting transfers between devices: 39.1 us -> none  [the longest x6 19.6 us: with_halo(): after = lax.ppermute(first, axis, down)]
    another operation x25 -> x0, other arithmetic: 20 us -> none  [the longest x15 10.7 us: solve_gram(): factor = jnp.linalg.cholesky(sym)]
    dot_general x17 -> x0, matrix products: 9.33 us -> none  [the longest x8 3.28 us: combine(): jnp.einsum('kxyz,kl->lxyz', values, coefs, precision=lax.Precision.HIGHEST)]
    ppermute x12 -> x0, waiting for transfers between devices: 6.8 us -> none  [the longest x6 5.29 us: with_halo(): before = lax.ppermute(last, axis, up)]
  transfers between devices with their start and end apart: 12 -> 0, of which waited for: 7 -> 0; matrix products, arithmetic and copies ran while one was open for 1% -> 0% of each run, Pallas kernels for 0% -> 0%
where the time goes in v1:
time: 60.7 us; the launch traced here: 60.5 us
  Pallas kernels  57.2 us (94%)
  local copies, waits for them, and re-layouts  2.71 us (4%)
  between operations  0.65 us (1%)
    pallas_call x1, Pallas kernels, on_device(): pl.pallas_call(functools.partial(kernel, n_wide, n_narrow), out_shape=(fi...  57.2 us
    unnamed x4, local copies, waits for them, and re-layouts  2.71 us

profile of v1, /device:TPU:1, one launch (start us, length us, event | category | flops | bytes accessed | tf_op | source)
XLA Modules:
  0.0 60.5 jit_solution(12270795415415674936)
XLA Ops:
  0.6 57.2 %shard_map.77 = (f32[2,8,16,256]{3,2,1,0:T(8,128)}, f32[2,8,16,256]{3,2,1,0:T(8,128)}) custom-call(f32[16,2,8,256]{3,2,1,0:T(8,128)} %src_hbm.1, s32[16]{0:T(128)} %wells_hbm.1, s32[2,8]{1,0:T(2,128)} %active_hbm.1, f32[2,8,256]{2,1,0:T(8,128)} %perm_hbm.1, f32[2,8,256]{2,1,0:T(8,128)} %storage_hbm.1, bf16[2,8,2,128,128]{4,3,2,1,0:T(8,128)(2,1)} %inv_hbm.1), custom_call_target="tpu_custom_call" | custom-call | tf_op jit(solution)/shard_map/pallas_call | solution.py:320
  57.8 0.0 copy-start
  57.8 1.9 %copy.8 = f32[16,2,8,256]{3,2,1,0:T(8,128)} copy(f32[16,2,8,256]{3,0,2,1:T(8,128)} %bitcast.3) | data formatting | bytes 524288
  59.7 0.0 copy-done
  59.7 0.9 %copy.9 = f32[16,2,8,256]{3,2,1,0:T(8,128)} copy(f32[16,2,8,256]{3,0,2,1:T(8,128)S(1)} %bitcast.2) | data formatting | bytes 524288
Async XLA Ops:
  57.8 1.9 %copy-start = (f32[2,8,16,256]{3,2,1,0:T(8,128)S(1)}, f32[2,8,16,256]{3,2,1,0:T(8,128)}, u32[]{:S(2)}) copy-start(f32[2,8,16,256]{3,2,1,0:T(8,128)} %get-tuple-element.5) | copy-start | bytes 786436

commit v2 on v1

--- a/solution.py
+++ b/solution.py
@@ -50,11 +50,15 @@
     halo_x,
     halo_y,
     part,
-    rows_in,
+    wide_in,
+    plane,
     plane_in,
-    plane,
-    all_rows,
-    total,
+    part_c,
+    wide_in_c,
+    plane_c,
+    plane_in_c,
+    matrix,
+    dfull,
     load_sem,
     coef_send,
     coef_recv,
@@ -112,9 +116,9 @@
     for load in loads[4:]:
         load.wait()
 
-    def precondition(get, put):
-        for x, y in columns:
-            value = get(x, y)
+    def precondition(source, i, x):
+        for y in range(cy):
+            value = source[x, y]
             high = value.astype(jnp.bfloat16)
             low = (value - high.astype(F32)).astype(jnp.bfloat16)
             both = jnp.concatenate([high, low], axis=0)
@@ -125,20 +129,16 @@
                     (((1,), (0,)), ((), ())),
                     preferred_element_type=F32,
                 )
-                put(x, y, b, out[:kk] + out[kk:])
+                out = out[:kk] + out[kk:]
+                zs[i, x, y, :, b * blk : (b + 1) * blk] = out if i == 0 else out * BASIS_SCALE
 
     first_x, first_y = me_w * cx, me_n * cy
     for x, y in columns:
         here = (first_x + x) * (n_narrow * cy) + first_y + y
         rhs[x, y] = rhs[x, y] + jnp.where(well_of == here, WELL_RATE, 0.0)
 
-    def store_z(i, scale):
-        def put(x, y, b, value):
-            zs[i, x, y, :, b * blk : (b + 1) * blk] = value * scale if scale != 1.0 else value
-
-        return put
-
-    precondition(lambda x, y: rhs[x, y], store_z(0, 1.0))
+    for x in range(cx):
+        precondition(rhs, 0, x)
 
     pl.semaphore_wait(barrier, n_narrow + n_wide - 2)
 
@@ -147,16 +147,13 @@
             src_ref=source, dst_ref=target, send_sem=send, recv_sem=recv, device_id=device, device_id_type=MESH
         )
 
-    def send_halo(i):
-        copies = [
+    def halo_copies(i):
+        return [
             remote(zs.at[i, cx - 1], halo_x.at[i, 0], halo_send.at[i, 0], halo_recv.at[i, 0], {"wide": right}),
             remote(zs.at[i, 0], halo_x.at[i, 1], halo_send.at[i, 1], halo_recv.at[i, 1], {"wide": left}),
             remote(zs.at[i, :, cy - 1], halo_y.at[i, 0], halo_send.at[i, 2], halo_recv.at[i, 2], {"narrow": above}),
             remote(zs.at[i, :, 0], halo_y.at[i, 1], halo_send.at[i, 3], halo_recv.at[i, 3], {"narrow": below}),
         ]
-        for copy in copies:
-            copy.start()
-        return copies
 
     coef_copies = [
         remote(coef.at[cx - 1], coef_x.at[0], coef_send.at[0], coef_recv.at[0], {"wide": right}),
@@ -166,7 +163,9 @@
     ]
     for copy in coef_copies:
         copy.start()
-    flying = send_halo(0)
+    flying = halo_copies(0)
+    for copy in flying:
+        copy.start()
 
     has_left = jnp.where(me_w == 0, 0.0, 1.0)
     has_right = jnp.where(me_w == n_wide - 1, 0.0, 1.0)
@@ -195,8 +194,6 @@
     def last_layer(value):
         return jnp.where(lane8 == 0, 0.0, pltpu.roll(value, 1, 1))
 
-    dfull = total
-
     def build_diag():
         for x, y in columns:
             c = coef_pad[x + 1, y + 1]
@@ -206,21 +203,39 @@
 
     build_diag()
 
-    def operate(i):
+    def operate_inside(i):
         for x, y in columns:
             c = coef_pad[x + 1, y + 1]
-            west, east = coef_pad[x, y + 1], coef_pad[x + 2, y + 1]
-            south, north = coef_pad[x + 1, y], coef_pad[x + 1, y + 2]
             for h in range(kk // 8):
                 ks = pl.ds(8 * h, 8)
                 v = zs[i, x, y, ks]
                 u = c * v
                 near = next_layer(u) + last_layer(u)
-                near += west * (zs[i, x - 1, y, ks] if x > 0 else halo_x[i, 0, y, ks])
-                near += east * (zs[i, x + 1, y, ks] if x < cx - 1 else halo_x[i, 1, y, ks])
-                near += south * (zs[i, x, y - 1, ks] if y > 0 else halo_y[i, 0, x, ks])
-                near += north * (zs[i, x, y + 1, ks] if y < cy - 1 else halo_y[i, 1, x, ks])
+                if x > 0:
+                    near += coef_pad[x, y + 1] * zs[i, x - 1, y, ks]
+                if x < cx - 1:
+                    near += coef_pad[x + 2, y + 1] * zs[i, x + 1, y, ks]
+                if y > 0:
+                    near += coef_pad[x + 1, y] * zs[i, x, y - 1, ks]
+                if y < cy - 1:
+                    near += coef_pad[x + 1, y + 2] * zs[i, x, y + 1, ks]
                 ws[i, x, y, ks] = dfull[x, y] * v - c * near
+
+    def operate_edge_y(i):
+        for x in range(cx):
+            for side, y, at in ((0, 0, 0), (1, cy - 1, cy + 1)):
+                both = coef_pad[x + 1, y + 1] * coef_pad[x + 1, at]
+                for h in range(kk // 8):
+                    ks = pl.ds(8 * h, 8)
+                    ws[i, x, y, ks] = ws[i, x, y, ks] - both * halo_y[i, side, x, ks]
+
+    def operate_edge_x(i):
+        for side, x, at in ((0, 0, 0), (1, cx - 1, cx + 1)):
+            for y in range(cy):
+                both = coef_pad[x + 1, y + 1] * coef_pad[at, y + 1]
+                for h in range(kk // 8):
+                    ks = pl.ds(8 * h, 8)
+                    ws[i, x, y, ks] = ws[i, x, y, ks] - both * halo_x[i, side, y, ks]
 
     def gram(lefts, rights):
         acc = None
@@ -231,74 +246,136 @@
             acc = product if acc is None else acc + product
         return acc
 
+    def send_all(axis, me, count, source, target, send, recv):
+        def send_to(d):
+            peer = lax.rem(me + d, count)
+            remote(source, target.at[d - 1], send, recv, {axis: peer}).start()
+
+        send_to(count // 2)
+
+        @pl.loop(1, count // 2)
+        def _(t):
+            send_to(count // 2 - t)
+            send_to(count // 2 + t)
+
+    def received(axis, peer, target, send, recv):
+        done = remote(target, target, send, recv, {axis: peer})
+        done.wait_recv()
+        done.wait_send()
+
+    def add_all(own, target):
+        lines = [own] + [target[d] for d in range(target.shape[0])]
+        while len(lines) > 1:
+            lines = [a + b for a, b in zip(lines[::2], lines[1::2])] + lines[len(lines) // 2 * 2 :]
+        return lines[0]
+
+    sums = [(part, wide_in, plane, plane_in), (part, wide_in, plane, plane_in), (part_c, wide_in_c, plane_c, plane_in_c)]
+    slot = [0, 1, 0]
+
+    def sum_wide(j, value):
+        own, into = sums[j][0].at[slot[j]], sums[j][1].at[slot[j]]
+        own[...] = value
+        send_all("wide", me_w, n_wide, own, into, sum_send.at[j, 0], sum_recv.at[j, 0])
+
+    def sum_narrow(j):
+        own, into, mid, last = (ref.at[slot[j]] for ref in sums[j])
+        received("wide", right, into, sum_send.at[j, 0], sum_recv.at[j, 0])
+        mid[...] = add_all(own[...], into)
+        send_all("narrow", me_n, n_narrow, mid, last, sum_send.at[j, 1], sum_recv.at[j, 1])
+
+    def sum_done(j):
+        mid, last = sums[j][2].at[slot[j]], sums[j][3].at[slot[j]]
+        received("narrow", above, last, sum_send.at[j, 1], sum_recv.at[j, 1])
+        return add_all(mid[...], last)
+
     z_refs = [zs.at[i] for i in range(BASIS)]
     w_refs = [ws.at[i] for i in range(BASIS)]
 
-    blocks = {}
+    def halve(line):
+        return jnp.concatenate([line[:8], line[8:]], axis=1)
+
     for i in range(BASIS):
         if i > 0:
-            precondition(lambda x, y: ws[i - 1, x, y], store_z(i, BASIS_SCALE))
-            flying = send_halo(i)
-        known = gram([rhs] + w_refs[:i], [z_refs[i]])
-        for r in range(i + 1):
-            blocks[r, i] = known[kk * r : kk * (r + 1)]
-        if i > 0:
-            mirror = gram([z_refs[i]], w_refs[:i])
-            for r in range(i):
-                blocks[i + 1, r] = mirror[:, kk * r : kk * (r + 1)]
-        for copy in flying:
+            flying = halo_copies(i)
+            for x in reversed(range(cx)):
+                precondition(w_refs[i - 1], i, x)
+                if x == cx - 1:
+                    flying[0].start()
+                if x == 0:
+                    flying[1].start()
+            flying[2].start()
+            flying[3].start()
+        operate_inside(i)
+        if i == 1:
+            first = gram([rhs, w_refs[0]], [z_refs[0], z_refs[1]])
+            sum_wide(0, halve(jnp.concatenate([first[:kk], first[kk:]], axis=1)))
+        if i == 2:
+            second = gram([rhs, w_refs[0], w_refs[1]], [z_refs[1], z_refs[2]])
+            line = [second[:kk, kk:], second[kk : 2 * kk, kk:], second[2 * kk :]]
+            sum_wide(1, halve(jnp.concatenate(line, axis=1)))
+            sum_narrow(0)
+        for copy in flying[2:]:
             copy.wait()
-        operate(i)
-        own = gram([w_refs[i]], [z_refs[i]])
-        blocks[i + 1, i] = own
-    half = (BASIS + 1) * kk // 2
-    span = BASIS * kk
-    pad = jnp.zeros((half, 64 - span), F32)
-    sums = jnp.concatenate(
-        [jnp.concatenate([blocks[r, i] for r in range(BASIS + 1)], axis=0) for i in range(BASIS)], axis=1
-    )
-    sums = jnp.concatenate([sums[:half], pad, sums[half:], pad], axis=1)
-    for r in range(half):
-        part[r] = sums[r : r + 1]
-
-    def start_all(axis, me, count, source, target, stage):
-        @pl.loop(1, count)
-        def _(d):
-            peer = lax.rem(me + d, count)
-            remote(source(peer), target(d), sum_send.at[stage], sum_recv.at[stage], {axis: peer}).start()
-
-    def wait_all(buffer, count, stage, axis, peer):
-        whole = buffer.at[pl.ds(0, count - 1)]
-        done = remote(whole, whole, sum_send.at[stage], sum_recv.at[stage], {axis: peer})
-        done.wait_send()
-        done.wait_recv()
-
-    start_all("wide", me_w, n_wide, lambda peer: part.at[peer], lambda d: rows_in.at[d - 1], 0)
-    mine = part[me_w]
-    wait_all(rows_in, n_wide, 0, "wide", right)
-    for d in range(n_wide - 1):
-        mine = mine + rows_in[d]
-    plane[...] = mine
-    start_all("narrow", me_n, n_narrow, lambda peer: plane, lambda d: plane_in.at[d - 1], 1)
-    wait_all(plane_in, n_narrow, 1, "narrow", above)
-    for d in range(n_narrow - 1):
-        mine = mine + plane_in[d]
-    all_rows[me_w] = mine
-    start_all("wide", me_w, n_wide, lambda peer: all_rows.at[me_w], lambda d: all_rows.at[me_w], 2)
-    wait_all(all_rows, n_wide, 2, "wide", right)
-
-    packed = jnp.concatenate([all_rows[r] for r in range(half)], axis=0)
-    low = packed
-    high = pltpu.roll(packed, 64, 1)
-    system = jnp.concatenate([low, high], axis=0)
-    lanes = lax.broadcasted_iota(jnp.int32, (1, 128), 1)
-    for k in range(span):
-        pivot_row = system[kk + k : kk + k + 1]
-        column = system[:, k : k + 1]
-        factor = pivot_row / pivot_row[:, k : k + 1]
-        inverse = 1.0 / pivot_row[:, k : k + 1]
-        system = jnp.where(lanes == k, column * inverse, system - column * factor)
-    y = system[:kk, :span]
+        operate_edge_y(i)
+        for copy in flying[:2]:
+            copy.wait()
+        operate_edge_x(i)
+
+    lanes = lax.broadcasted_iota(jnp.int32, (kk, 128), 1)
+    rows = lax.broadcasted_iota(jnp.int32, (kk, 128), 0)
+    diagonal = lanes // kk == lax.rem(rows, 8)
+    third = gram([w_refs[2]], [z_refs[2]])
+    third = jnp.where(diagonal, jnp.concatenate([third] * 8, axis=1), 0.0)
+    sum_wide(2, jnp.concatenate([jnp.sum(third[:8], axis=0, keepdims=True), jnp.sum(third[8:], axis=0, keepdims=True)], axis=0))
+
+    matrix[...] = jnp.zeros_like(matrix)
+    sum_narrow(1)
+    first = sum_done(0)
+    for h in range(2):
+        matrix[8 * h : 8 * h + 8, 0 : 2 * kk] = first[:, 64 * h : 64 * h + 2 * kk]
+        matrix[kk + 8 * h : kk + 8 * h + 8, 0 : 2 * kk] = first[:, 64 * h + 2 * kk : 64 * h + 4 * kk]
+    sum_narrow(2)
+    second = sum_done(1)
+    for h in range(2):
+        for r in range(2):
+            piece = second[:, 64 * h + r * kk : 64 * h + (r + 1) * kk]
+            matrix[r * kk + 8 * h : r * kk + 8 * h + 8, 2 * kk : 3 * kk] = piece
+        matrix[2 * kk + 8 * h : 2 * kk + 8 * h + 8, kk : 3 * kk] = second[:, 64 * h + 2 * kk : 64 * h + 4 * kk]
+    pick_rows = lax.broadcasted_iota(jnp.int32, (2 * kk, 128), 0)
+    pick_lanes = lax.broadcasted_iota(jnp.int32, (2 * kk, 128), 1)
+    pick = jnp.where(pick_lanes == pick_rows + kk, 1.0, 0.0)
+    matrix[2 * kk :, 0 : 2 * kk] = dot_nt(pick, matrix[kk : 3 * kk])
+
+    lane = lax.broadcasted_iota(jnp.int32, (1, 128), 1)
+
+    def eliminate(system, row, k):
+        shape = system.shape
+        c0 = jnp.broadcast_to(system[:, k : k + 1], shape)
+        c1 = jnp.broadcast_to(system[:, k + 1 : k + 2], shape)
+        p0, p1 = system[row : row + 1], system[row + 1 : row + 2]
+        a, b = c0[row : row + 1], c1[row : row + 1]
+        c, d = c0[row + 1 : row + 2], c1[row + 1 : row + 2]
+        inverse = 1.0 / (a * d - b * c)
+        at0, at1 = lane == k, lane == k + 1
+        g0 = jnp.where(at0, -d, jnp.where(at1, b, d * p0 - b * p1)) * inverse
+        g1 = jnp.where(at0, c, jnp.where(at1, -a, a * p1 - c * p0)) * inverse
+        kept = jnp.where(at0 | at1, 0.0, system)
+        return kept - c0 * g0 - c1 * g1
+
+    system = matrix[...]
+    for k in range(0, 2 * kk, 2):
+        system = eliminate(system, kk + k, k)
+
+    third = sum_done(2)
+    third = jnp.concatenate([jnp.broadcast_to(third[h : h + 1], (8, 128)) for h in range(2)], axis=0)
+    third = jnp.where(diagonal, third, 0.0)
+    for shift in (64, 32, 16):
+        third = third + pltpu.roll(third, shift, 1)
+    third = jnp.where((lanes >= 2 * kk) & (lanes < 3 * kk), third, 0.0)
+    system = jnp.concatenate([system[:kk], system[3 * kk :] + third], axis=0)
+    for k in range(0, kk, 2):
+        system = eliminate(system, kk + k, 2 * kk + k)
+    y = system[:kk, : BASIS * kk]
 
     for x, yy in columns:
         basis = jnp.concatenate([zs[i, x, yy] for i in range(BASIS)], axis=0)
@@ -313,7 +390,6 @@
     def on_device(sources, well_columns, column_active, perm_root, storage_term, inverse_blocks):
         kk, cx, cy, nz = sources.shape
         nb, blk = inverse_blocks.shape[2], inverse_blocks.shape[3]
-        rows = (BASIS + 1) * kk // 2
         field = jax.ShapeDtypeStruct((cx, cy, kk, nz), F32)
         dma = pltpu.SemaphoreType.DMA
         vmem = pltpu.VMEM
@@ -338,19 +414,23 @@
                 vmem((BASIS, cx, cy, kk, nz), F32),
                 vmem((BASIS, 2, cy, kk, nz), F32),
                 vmem((BASIS, 2, cx, kk, nz), F32),
-                vmem((rows, 1, 128), F32),
-                vmem((n_wide - 1, 1, 128), F32),
-                vmem((n_narrow - 1, 1, 128), F32),
-                vmem((1, 128), F32),
-                vmem((rows, 1, 128), F32),
+                vmem((2, 8, 128), F32),
+                vmem((2, n_wide - 1, 8, 128), F32),
+                vmem((2, 8, 128), F32),
+                vmem((2, n_narrow - 1, 8, 128), F32),
+                vmem((1, 2, 128), F32),
+                vmem((1, n_wide - 1, 2, 128), F32),
+                vmem((1, 2, 128), F32),
+                vmem((1, n_narrow - 1, 2, 128), F32),
+                vmem(((BASIS + 1) * kk, 128), F32),
                 vmem((cx, cy, 8, nz), F32),
                 dma((5 + cx * cy,)),
                 dma((4,)),
                 dma((4,)),
                 dma((BASIS, 4)),
                 dma((BASIS, 4)),
-                dma((3,)),
-                dma((3,)),
+                dma((3, 2)),
+                dma((3, 2)),
             ],
             compiler_params=pltpu.CompilerParams(collective_id=0, has_side_effects=True),
         )(sources, well_columns, column_active, perm_root, storage_term, inverse_blocks)

time: 60.7 us -> 52.4 us (0.86)
  Pallas kernels: 57.2 us -> 48.9 us
    pallas_call x1, Pallas kernels: 57.2 us -> 48.9 us  [on_device(): pl.pallas_call(functools.partial(kernel, n_wide, n_narrow), out_shape=(fi...]
where the time goes in v2:
time: 52.4 us; the launch traced here: 52.2 us
  Pallas kernels  48.9 us (93%)
  local copies, waits for them, and re-layouts  2.71 us (5%)
  between operations  0.65 us (1%)
    pallas_call x1, Pallas kernels, on_device(): pl.pallas_call(functools.partial(kernel, n_wide, n_narrow), out_shape=(fi...  48.9 us
    unnamed x4, local copies, waits for them, and re-layouts  2.71 us

profile of v2, /device:TPU:1, one launch (start us, length us, event | category | flops | bytes accessed | tf_op | source)
XLA Modules:
  0.0 52.2 jit_solution(14908386859890174112)
XLA Ops:
  0.6 48.9 %shard_map.77 = (f32[2,8,16,256]{3,2,1,0:T(8,128)}, f32[2,8,16,256]{3,2,1,0:T(8,128)}) custom-call(f32[16,2,8,256]{3,2,1,0:T(8,128)} %src_hbm.1, s32[16]{0:T(128)} %wells_hbm.1, s32[2,8]{1,0:T(2,128)} %active_hbm.1, f32[2,8,256]{2,1,0:T(8,128)} %perm_hbm.1, f32[2,8,256]{2,1,0:T(8,128)} %storage_hbm.1, bf16[2,8,2,128,128]{4,3,2,1,0:T(8,128)(2,1)} %inv_hbm.1), custom_call_target="tpu_custom_call" | custom-call | tf_op jit(solution)/shard_map/pallas_call | solution.py:396
  49.5 0.0 copy-start
  49.5 1.9 %copy.8 = f32[16,2,8,256]{3,2,1,0:T(8,128)} copy(f32[16,2,8,256]{3,0,2,1:T(8,128)} %bitcast.3) | data formatting | bytes 524288
  51.4 0.0 copy-done
  51.4 0.9 %copy.9 = f32[16,2,8,256]{3,2,1,0:T(8,128)} copy(f32[16,2,8,256]{3,0,2,1:T(8,128)S(1)} %bitcast.2) | data formatting | bytes 524288
Async XLA Ops:
  49.5 1.9 %copy-start = (f32[2,8,16,256]{3,2,1,0:T(8,128)S(1)}, f32[2,8,16,256]{3,2,1,0:T(8,128)}, u32[]{:S(2)}) copy-start(f32[2,8,16,256]{3,2,1,0:T(8,128)} %get-tuple-element.5) | copy-start | bytes 786436

commit v3 on v2

--- a/solution.py
+++ b/solution.py
@@ -12,15 +12,17 @@
 BASIS_SCALE = 1.0 / 16.0
 MESH = pl.DeviceIdType.MESH
 EXACT = lax.Precision.HIGHEST
+SPLIT = lax.Precision.HIGH
+CHUNKS = 4
 F32 = jnp.float32
 
 
-def dot_nt(left, right):
-    return lax.dot_general(left, right, (((1,), (1,)), ((), ())), precision=EXACT, preferred_element_type=F32)
+def dot_nt(left, right, precision=EXACT):
+    return lax.dot_general(left, right, (((1,), (1,)), ((), ())), precision=precision, preferred_element_type=F32)
 
 
 def dot_nn(left, right):
-    return lax.dot_general(left, right, (((1,), (0,)), ((), ())), precision=EXACT, preferred_element_type=F32)
+    return lax.dot_general(left, right, (((1,), (0,)), ((), ())), precision=SPLIT, preferred_element_type=F32)
 
 
 def kernel(
@@ -32,9 +34,10 @@
     perm_hbm,
     storage_hbm,
     inv_hbm,
-    sol_ref,
-    res_ref,
+    weights,
     rhs,
+    zs,
+    ws,
     wells,
     active,
     perm,
@@ -45,8 +48,6 @@
     coef_x,
     coef_pad,
     diag,
-    zs,
-    ws,
     halo_x,
     halo_y,
     part,
@@ -116,8 +117,14 @@
     for load in loads[4:]:
         load.wait()
 
-    def precondition(source, i, x):
-        for y in range(cy):
+    wide_y = cy // CHUNKS
+    order = [0, CHUNKS - 1] + list(range(1, CHUNKS - 1))
+
+    def chunk(c):
+        return [(x, y) for x in reversed(range(cx)) for y in range(c * wide_y, (c + 1) * wide_y)]
+
+    def precondition(source, i, c):
+        for x, y in chunk(c):
             value = source[x, y]
             high = value.astype(jnp.bfloat16)
             low = (value - high.astype(F32)).astype(jnp.bfloat16)
@@ -137,8 +144,8 @@
         here = (first_x + x) * (n_narrow * cy) + first_y + y
         rhs[x, y] = rhs[x, y] + jnp.where(well_of == here, WELL_RATE, 0.0)
 
-    for x in range(cx):
-        precondition(rhs, 0, x)
+    for c in order:
+        precondition(rhs, 0, c)
 
     pl.semaphore_wait(barrier, n_narrow + n_wide - 2)
 
@@ -147,13 +154,23 @@
             src_ref=source, dst_ref=target, send_sem=send, recv_sem=recv, device_id=device, device_id_type=MESH
         )
 
-    def halo_copies(i):
-        return [
-            remote(zs.at[i, cx - 1], halo_x.at[i, 0], halo_send.at[i, 0], halo_recv.at[i, 0], {"wide": right}),
-            remote(zs.at[i, 0], halo_x.at[i, 1], halo_send.at[i, 1], halo_recv.at[i, 1], {"wide": left}),
-            remote(zs.at[i, :, cy - 1], halo_y.at[i, 0], halo_send.at[i, 2], halo_recv.at[i, 2], {"narrow": above}),
-            remote(zs.at[i, :, 0], halo_y.at[i, 1], halo_send.at[i, 3], halo_recv.at[i, 3], {"narrow": below}),
-        ]
+    def copy_x(i, side, c):
+        ys = pl.ds(c * wide_y, wide_y)
+        source, device = ((cx - 1, {"wide": right}), (0, {"wide": left}))[side]
+        send, recv = halo_send.at[i, 2 + 2 * c + side], halo_recv.at[i, 2 + 2 * c + side]
+        return remote(zs.at[i, source, ys], halo_x.at[i, side, ys], send, recv, device)
+
+    def copy_y(i, side):
+        source, device = ((cy - 1, {"narrow": above}), (0, {"narrow": below}))[side]
+        return remote(zs.at[i, :, source], halo_y.at[i, side], halo_send.at[i, side], halo_recv.at[i, side], device)
+
+    def emit(i, c):
+        copy_x(i, 0, c).start()
+        copy_x(i, 1, c).start()
+        if c == CHUNKS - 1:
+            copy_y(i, 0).start()
+        if c == 0:
+            copy_y(i, 1).start()
 
     coef_copies = [
         remote(coef.at[cx - 1], coef_x.at[0], coef_send.at[0], coef_recv.at[0], {"wide": right}),
@@ -163,9 +180,8 @@
     ]
     for copy in coef_copies:
         copy.start()
-    flying = halo_copies(0)
-    for copy in flying:
-        copy.start()
+    for c in order:
+        emit(0, c)
 
     has_left = jnp.where(me_w == 0, 0.0, 1.0)
     has_right = jnp.where(me_w == n_wide - 1, 0.0, 1.0)
@@ -177,15 +193,6 @@
 
     for x, y in columns:
         coef_pad[x + 1, y + 1] = spread(coef[x, y : y + 1])
-    for copy in coef_copies:
-        copy.wait()
-    for y in range(cy):
-        coef_pad[0, y + 1] = spread(coef_x[0, y : y + 1] * has_left)
-        coef_pad[cx + 1, y + 1] = spread(coef_x[1, y : y + 1] * has_right)
-    for x in range(cx):
-        coef_pad[x + 1, 0] = spread(coef_y[0, x, cy - 1 : cy] * has_below)
-        coef_pad[x + 1, cy + 1] = spread(coef_y[1, x, 0:1] * has_above)
-
     lane8 = lax.broadcasted_iota(jnp.int32, (8, nz), 1)
 
     def next_layer(value):
@@ -194,14 +201,22 @@
     def last_layer(value):
         return jnp.where(lane8 == 0, 0.0, pltpu.roll(value, 1, 1))
 
-    def build_diag():
-        for x, y in columns:
-            c = coef_pad[x + 1, y + 1]
-            around = coef_pad[x, y + 1] + coef_pad[x + 2, y + 1] + coef_pad[x + 1, y] + coef_pad[x + 1, y + 2]
-            around += next_layer(c) + last_layer(c)
-            dfull[x, y] = spread(diag[x, y : y + 1]) + c * around
-
-    build_diag()
+    def coupled(x, y):
+        if x > 0:
+            yield (x, y + 1), (x - 1, y)
+        if x < cx - 1:
+            yield (x + 2, y + 1), (x + 1, y)
+        if y > 0:
+            yield (x + 1, y), (x, y - 1)
+        if y < cy - 1:
+            yield (x + 1, y + 2), (x, y + 1)
+
+    for x, y in columns:
+        c = coef_pad[x + 1, y + 1]
+        around = next_layer(c) + last_layer(c)
+        for at, _ in coupled(x, y):
+            around += coef_pad[at]
+        dfull[x, y] = spread(diag[x, y : y + 1]) + c * around
 
     def operate_inside(i):
         for x, y in columns:
@@ -211,38 +226,41 @@
                 v = zs[i, x, y, ks]
                 u = c * v
                 near = next_layer(u) + last_layer(u)
-                if x > 0:
-                    near += coef_pad[x, y + 1] * zs[i, x - 1, y, ks]
-                if x < cx - 1:
-                    near += coef_pad[x + 2, y + 1] * zs[i, x + 1, y, ks]
-                if y > 0:
-                    near += coef_pad[x + 1, y] * zs[i, x, y - 1, ks]
-                if y < cy - 1:
-                    near += coef_pad[x + 1, y + 2] * zs[i, x, y + 1, ks]
+                for at, (nx, ny) in coupled(x, y):
+                    near += coef_pad[at] * zs[i, nx, ny, ks]
                 ws[i, x, y, ks] = dfull[x, y] * v - c * near
 
-    def operate_edge_y(i):
-        for x in range(cx):
-            for side, y, at in ((0, 0, 0), (1, cy - 1, cy + 1)):
-                both = coef_pad[x + 1, y + 1] * coef_pad[x + 1, at]
-                for h in range(kk // 8):
-                    ks = pl.ds(8 * h, 8)
-                    ws[i, x, y, ks] = ws[i, x, y, ks] - both * halo_y[i, side, x, ks]
-
-    def operate_edge_x(i):
-        for side, x, at in ((0, 0, 0), (1, cx - 1, cx + 1)):
-            for y in range(cy):
-                both = coef_pad[x + 1, y + 1] * coef_pad[at, y + 1]
-                for h in range(kk // 8):
-                    ks = pl.ds(8 * h, 8)
-                    ws[i, x, y, ks] = ws[i, x, y, ks] - both * halo_x[i, side, y, ks]
+    def absorb(i, c):
+        copy_x(i, 0, c).wait()
+        copy_x(i, 1, c).wait()
+        if c == 0:
+            copy_y(i, 0).wait()
+        if c == CHUNKS - 1:
+            copy_y(i, 1).wait()
+        for x, y in chunk(c):
+            edges = []
+            if x == 0:
+                edges.append(((0, y + 1), halo_x.at[i, 0, y]))
+            if x == cx - 1:
+                edges.append(((cx + 1, y + 1), halo_x.at[i, 1, y]))
+            if y == 0:
+                edges.append(((x + 1, 0), halo_y.at[i, 0, x]))
+            if y == cy - 1:
+                edges.append(((x + 1, cy + 1), halo_y.at[i, 1, x]))
+            both = [coef_pad[x + 1, y + 1] * coef_pad[at] for at, _ in edges]
+            for h in range(kk // 8):
+                ks = pl.ds(8 * h, 8)
+                v, w = zs[i, x, y, ks], ws[i, x, y, ks]
+                for pair, (_, outer) in zip(both, edges):
+                    w += pair * (v - outer[ks])
+                ws[i, x, y, ks] = w
 
     def gram(lefts, rights):
         acc = None
         for x, y in columns:
             left_rows = jnp.concatenate([ref[x, y] for ref in lefts], axis=0)
             right_rows = jnp.concatenate([ref[x, y] for ref in rights], axis=0)
-            product = dot_nt(left_rows, right_rows)
+            product = dot_nt(left_rows, right_rows, SPLIT)
             acc = product if acc is None else acc + product
         return acc
 
@@ -296,16 +314,20 @@
 
     for i in range(BASIS):
         if i > 0:
-            flying = halo_copies(i)
-            for x in reversed(range(cx)):
-                precondition(w_refs[i - 1], i, x)
-                if x == cx - 1:
-                    flying[0].start()
-                if x == 0:
-                    flying[1].start()
-            flying[2].start()
-            flying[3].start()
+            for c in order:
+                absorb(i - 1, c)
+                precondition(w_refs[i - 1], i, c)
+                emit(i, c)
         operate_inside(i)
+        if i == 0:
+            for copy in coef_copies:
+                copy.wait()
+            for y in range(cy):
+                coef_pad[0, y + 1] = spread(coef_x[0, y : y + 1] * has_left)
+                coef_pad[cx + 1, y + 1] = spread(coef_x[1, y : y + 1] * has_right)
+            for x in range(cx):
+                coef_pad[x + 1, 0] = spread(coef_y[0, x, cy - 1 : cy] * has_below)
+                coef_pad[x + 1, cy + 1] = spread(coef_y[1, x, 0:1] * has_above)
         if i == 1:
             first = gram([rhs, w_refs[0]], [z_refs[0], z_refs[1]])
             sum_wide(0, halve(jnp.concatenate([first[:kk], first[kk:]], axis=1)))
@@ -314,12 +336,8 @@
             line = [second[:kk, kk:], second[kk : 2 * kk, kk:], second[2 * kk :]]
             sum_wide(1, halve(jnp.concatenate(line, axis=1)))
             sum_narrow(0)
-        for copy in flying[2:]:
-            copy.wait()
-        operate_edge_y(i)
-        for copy in flying[:2]:
-            copy.wait()
-        operate_edge_x(i)
+    for c in order:
+        absorb(BASIS - 1, c)
 
     lanes = lax.broadcasted_iota(jnp.int32, (kk, 128), 1)
     rows = lax.broadcasted_iota(jnp.int32, (kk, 128), 0)
@@ -375,13 +393,25 @@
     system = jnp.concatenate([system[:kk], system[3 * kk :] + third], axis=0)
     for k in range(0, kk, 2):
         system = eliminate(system, kk + k, 2 * kk + k)
-    y = system[:kk, : BASIS * kk]
-
-    for x, yy in columns:
-        basis = jnp.concatenate([zs[i, x, yy] for i in range(BASIS)], axis=0)
-        image = jnp.concatenate([ws[i, x, yy] for i in range(BASIS)], axis=0)
-        sol_ref[x, yy] = dot_nn(y, basis)
-        res_ref[x, yy] = rhs[x, yy] - dot_nn(y, image)
+    weights[...] = system[:kk]
+
+
+def combine(weights, rhs, zs, ws, sol_hbm, res_hbm, sol, res, out_sem):
+    cx, cy, kk, nz = rhs.shape
+    y = weights[:, : BASIS * kk]
+    copies = []
+    for x in range(cx):
+        for yy in range(cy):
+            basis = jnp.concatenate([zs[i, x, yy] for i in range(BASIS)], axis=0)
+            image = jnp.concatenate([ws[i, x, yy] for i in range(BASIS)], axis=0)
+            sol[x, yy] = dot_nn(y, basis)
+            res[x, yy] = rhs[x, yy] - dot_nn(y, image)
+            for buffer, target in ((sol, sol_hbm), (res, res_hbm)):
+                copy = pltpu.make_async_copy(buffer.at[x, yy], target.at[:, x, yy, :], out_sem.at[len(copies)])
+                copy.start()
+                copies.append(copy)
+    for copy in copies:
+        copy.wait()
 
 
 def solution(mesh):
@@ -390,16 +420,19 @@
     def on_device(sources, well_columns, column_active, perm_root, storage_term, inverse_blocks):
         kk, cx, cy, nz = sources.shape
         nb, blk = inverse_blocks.shape[2], inverse_blocks.shape[3]
-        field = jax.ShapeDtypeStruct((cx, cy, kk, nz), F32)
         dma = pltpu.SemaphoreType.DMA
         vmem = pltpu.VMEM
-        out = pl.pallas_call(
+        held = pl.pallas_call(
             functools.partial(kernel, n_wide, n_narrow),
-            out_shape=(field, field),
+            out_shape=(
+                vmem((kk, 128), F32),
+                vmem((cx, cy, kk, nz), F32),
+                vmem((BASIS, cx, cy, kk, nz), F32),
+                vmem((BASIS, cx, cy, kk, nz), F32),
+            ),
             in_specs=[pl.BlockSpec(memory_space=pl.ANY)] * 6,
-            out_specs=(pl.BlockSpec(memory_space=vmem),) * 2,
+            out_specs=(pl.BlockSpec(memory_space=vmem),) * 4,
             scratch_shapes=[
-                vmem((cx, cy, kk, nz), F32),
                 pltpu.SMEM(well_columns.shape, jnp.int32),
                 pltpu.SMEM(column_active.shape, jnp.int32),
                 vmem((cx, cy, nz), F32),
@@ -410,8 +443,6 @@
                 vmem((2, cy, nz), F32),
                 vmem((cx + 2, cy + 2, 8, nz), F32),
                 vmem((cx, cy, nz), F32),
-                vmem((BASIS, cx, cy, kk, nz), F32),
-                vmem((BASIS, cx, cy, kk, nz), F32),
                 vmem((BASIS, 2, cy, kk, nz), F32),
                 vmem((BASIS, 2, cx, kk, nz), F32),
                 vmem((2, 8, 128), F32),
@@ -427,14 +458,25 @@
                 dma((5 + cx * cy,)),
                 dma((4,)),
                 dma((4,)),
-                dma((BASIS, 4)),
-                dma((BASIS, 4)),
+                dma((BASIS, 2 + 2 * CHUNKS)),
+                dma((BASIS, 2 + 2 * CHUNKS)),
                 dma((3, 2)),
                 dma((3, 2)),
             ],
             compiler_params=pltpu.CompilerParams(collective_id=0, has_side_effects=True),
         )(sources, well_columns, column_active, perm_root, storage_term, inverse_blocks)
-        return tuple(jnp.transpose(value, (2, 0, 1, 3)) for value in out)
+        field = jax.ShapeDtypeStruct(sources.shape, F32)
+        return pl.pallas_call(
+            combine,
+            out_shape=(field, field),
+            in_specs=[pl.BlockSpec(memory_space=vmem)] * 4,
+            out_specs=(pl.BlockSpec(memory_space=pl.ANY),) * 2,
+            scratch_shapes=[
+                vmem((cx, cy, kk, nz), F32),
+                vmem((cx, cy, kk, nz), F32),
+                dma((2 * cx * cy,)),
+            ],
+        )(*(pltpu.with_memory_space_constraint(value, vmem) for value in held))
 
     in_specs = (
         P(None, "wide", "narrow", None),

time: 52.4 us -> 47.9 us (0.914)
  local copies, waits for them, and re-layouts: 2.71 us -> 0 us
  Pallas kernels: 48.9 us -> 47.1 us
    unnamed x4 -> x0, local copies, waits for them, and re-layouts: 2.71 us -> none
    pallas_call x1 -> x2, Pallas kernels: 48.9 us -> 47.1 us  [the longest x1 43.9 us: on_device(): pl.pallas_call(functools.partial(kernel, n_wide, n_narrow), out_shape=(vm...]
where the time goes in v3:
time: 47.9 us; the launch traced here: 47.8 us
  Pallas kernels  47.1 us (98%)
  between operations  0.64 us (1%)
    pallas_call x1, Pallas kernels, on_device(): pl.pallas_call(functools.partial(kernel, n_wide, n_narrow), out_shape=(vm...  43.9 us
    pallas_call x1, Pallas kernels, on_device(): pl.pallas_call(combine, out_shape=(field, field), in_specs=[pl.BlockSpec(...  3.26 us

profile of v3, /device:TPU:1, one launch (start us, length us, event | category | flops | bytes accessed | tf_op | source)
XLA Modules:
  0.0 47.8 jit_solution(12110651255319766257)
XLA Ops:
  0.6 43.9 %shard_map.77 = (f32[16,128]{1,0:T(8,128)S(1)}, f32[2,8,16,256]{3,2,1,0:T(8,128)S(1)}, f32[3,2,8,16,256]{4,3,2,1,0:T(8,128)S(1)}, f32[3,2,8,16,256]{4,3,2,1,0:T(8,128)S(1)}) custom-call(f32[16,2,8,256]{3,2,1,0:T(8,128)} %src_hbm.1, s32[16]{0:T(128)} %wells_hbm.1, s32[2,8]{1,0:T(2,128)} %active_hbm.1, f32[2,8,256]{2,1,0:T(8,128)} %perm_hbm.1, ...), custom_call_target="tpu_custom_call" | custom-call | tf_op jit(solution)/shard_map/pallas_call | solution.py:425
  44.5 3.3 %shard_map.78 = (f32[16,2,8,256]{3,2,1,0:T(8,128)}, f32[16,2,8,256]{3,2,1,0:T(8,128)}) custom-call(f32[16,128]{1,0:T(8,128)S(1)} %get-tuple-element.6.weights, f32[2,8,16,256]{3,2,1,0:T(8,128)S(1)} %get-tuple-element.7.rhs, f32[3,2,8,16,256]{4,3,2,1,0:T(8,128)S(1)} %get-tuple-element.8.zs, f32[3,2,8,16,256]{4,3,2,1,0:T(8,128)S(1)} %get-tuple-element.9.ws), custom_call_target="tpu_custom_call" | custom-call | tf_op jit(solution)/shard_map/pallas_call | solution.py:469

commit v4 on v3

--- a/solution.py
+++ b/solution.py
@@ -67,6 +67,7 @@
     halo_recv,
     sum_send,
     sum_recv,
+    tokens,
 ):
     kk, cx, cy, nz = src_hbm.shape
     blk = inv_hbm.shape[-1]
@@ -77,29 +78,48 @@
 
     barrier = pltpu.get_barrier_semaphore()
 
-    @pl.loop(1, n_narrow)
-    def _(d):
-        peer = lax.rem(me_n + d, n_narrow)
-        pl.semaphore_signal(barrier, inc=1, device_id={"narrow": peer}, device_id_type=MESH)
-
-    @pl.loop(1, n_wide)
-    def _(d):
-        peer = lax.rem(me_w + d, n_wide)
-        pl.semaphore_signal(barrier, inc=1, device_id={"wide": peer}, device_id_type=MESH)
+    for axis, peer in (("wide", right), ("wide", left), ("narrow", above), ("narrow", below)):
+        pl.semaphore_signal(barrier, inc=1, device_id={axis: peer}, device_id_type=MESH)
+
+    rings = {"wide": (0, me_w, n_wide), "narrow": (1, me_n, n_narrow)}
+
+    def tell(axis, r):
+        at, me, count = rings[axis]
+        for d in (2**r, count - 2**r):
+            peer = lax.rem(me + d, count)
+            pl.semaphore_signal(tokens.at[at, r], inc=1, device_id={axis: peer}, device_id_type=MESH)
+
+    def hear(axis, r):
+        pl.semaphore_wait(tokens.at[rings[axis][0], r], 2)
 
     loads = [
         pltpu.make_async_copy(wells_hbm, wells, load_sem.at[0]),
         pltpu.make_async_copy(active_hbm, active, load_sem.at[1]),
         pltpu.make_async_copy(perm_hbm, perm, load_sem.at[2]),
         pltpu.make_async_copy(storage_hbm, storage, load_sem.at[3]),
-        pltpu.make_async_copy(inv_hbm, inv, load_sem.at[4]),
     ]
+    wide_y = cy // CHUNKS
+    order = [0, CHUNKS - 1] + list(range(1, CHUNKS - 1))
+
+    def chunk(c):
+        return [(x, y) for x in reversed(range(cx)) for y in range(c * wide_y, (c + 1) * wide_y)]
+
     columns = [(x, y) for x in range(cx) for y in range(cy)]
-    for at, (x, y) in enumerate(columns):
-        loads.append(pltpu.make_async_copy(src_hbm.at[:, x, y, :], rhs.at[x, y], load_sem.at[5 + at]))
+    chunk_loads = {}
+    for c in order:
+        ys = pl.ds(c * wide_y, wide_y)
+        own = [(inv_hbm.at[x, ys], inv.at[x, ys]) for x in range(cx)]
+        own += [(src_hbm.at[:, x, y, :], rhs.at[x, y]) for x, y in chunk(c)]
+        first = 4 + c * len(own)
+        chunk_loads[c] = [
+            pltpu.make_async_copy(source, target, load_sem.at[first + at]) for at, (source, target) in enumerate(own)
+        ]
+    for load in loads + [load for c in order for load in chunk_loads[c]]:
+        load.start()
+    pl.semaphore_wait(barrier, 4)
+    tell("wide", 0)
+    tell("narrow", 0)
     for load in loads:
-        load.start()
-    for load in loads[:4]:
         load.wait()
 
     row = lax.broadcasted_iota(jnp.int32, (cy, nz), 0)
@@ -114,14 +134,6 @@
     well_of = jnp.zeros((kk, nz), jnp.int32)
     for k in range(kk):
         well_of = jnp.where(ids == k, wells[k], well_of)
-    for load in loads[4:]:
-        load.wait()
-
-    wide_y = cy // CHUNKS
-    order = [0, CHUNKS - 1] + list(range(1, CHUNKS - 1))
-
-    def chunk(c):
-        return [(x, y) for x in reversed(range(cx)) for y in range(c * wide_y, (c + 1) * wide_y)]
 
     def precondition(source, i, c):
         for x, y in chunk(c):
@@ -140,15 +152,6 @@
                 zs[i, x, y, :, b * blk : (b + 1) * blk] = out if i == 0 else out * BASIS_SCALE
 
     first_x, first_y = me_w * cx, me_n * cy
-    for x, y in columns:
-        here = (first_x + x) * (n_narrow * cy) + first_y + y
-        rhs[x, y] = rhs[x, y] + jnp.where(well_of == here, WELL_RATE, 0.0)
-
-    for c in order:
-        precondition(rhs, 0, c)
-
-    pl.semaphore_wait(barrier, n_narrow + n_wide - 2)
-
     def remote(source, target, send, recv, device):
         return pltpu.make_async_remote_copy(
             src_ref=source, dst_ref=target, send_sem=send, recv_sem=recv, device_id=device, device_id_type=MESH
@@ -181,7 +184,16 @@
     for copy in coef_copies:
         copy.start()
     for c in order:
+        for load in chunk_loads[c]:
+            load.wait()
+        for x, y in chunk(c):
+            here = (first_x + x) * (n_narrow * cy) + first_y + y
+            rhs[x, y] = rhs[x, y] + jnp.where(well_of == here, WELL_RATE, 0.0)
+        precondition(rhs, 0, c)
         emit(0, c)
+    for axis in ("wide", "narrow"):
+        hear(axis, 0)
+        tell(axis, 1)
 
     has_left = jnp.where(me_w == 0, 0.0, 1.0)
     has_right = jnp.where(me_w == n_wide - 1, 0.0, 1.0)
@@ -318,6 +330,11 @@
                 absorb(i - 1, c)
                 precondition(w_refs[i - 1], i, c)
                 emit(i, c)
+        if i == 1:
+            hear("wide", 2)
+            tell("wide", 3)
+            hear("narrow", 1)
+            tell("narrow", 2)
         operate_inside(i)
         if i == 0:
             for copy in coef_copies:
@@ -328,13 +345,18 @@
             for x in range(cx):
                 coef_pad[x + 1, 0] = spread(coef_y[0, x, cy - 1 : cy] * has_below)
                 coef_pad[x + 1, cy + 1] = spread(coef_y[1, x, 0:1] * has_above)
+        if i == 0:
+            hear("wide", 1)
+            tell("wide", 2)
         if i == 1:
             first = gram([rhs, w_refs[0]], [z_refs[0], z_refs[1]])
+            hear("wide", 3)
             sum_wide(0, halve(jnp.concatenate([first[:kk], first[kk:]], axis=1)))
         if i == 2:
             second = gram([rhs, w_refs[0], w_refs[1]], [z_refs[1], z_refs[2]])
             line = [second[:kk, kk:], second[kk : 2 * kk, kk:], second[2 * kk :]]
             sum_wide(1, halve(jnp.concatenate(line, axis=1)))
+            hear("narrow", 2)
             sum_narrow(0)
     for c in order:
         absorb(BASIS - 1, c)
@@ -396,7 +418,7 @@
     weights[...] = system[:kk]
 
 
-def combine(weights, rhs, zs, ws, sol_hbm, res_hbm, sol, res, out_sem):
+def combine(weights, rhs, zs, ws, sol_hbm, res_hbm, sol, res, sol_turned, res_turned, out_sem):
     cx, cy, kk, nz = rhs.shape
     y = weights[:, : BASIS * kk]
     copies = []
@@ -406,10 +428,11 @@
             image = jnp.concatenate([ws[i, x, yy] for i in range(BASIS)], axis=0)
             sol[x, yy] = dot_nn(y, basis)
             res[x, yy] = rhs[x, yy] - dot_nn(y, image)
-            for buffer, target in ((sol, sol_hbm), (res, res_hbm)):
-                copy = pltpu.make_async_copy(buffer.at[x, yy], target.at[:, x, yy, :], out_sem.at[len(copies)])
-                copy.start()
-                copies.append(copy)
+        for buffer, turned, target in ((sol, sol_turned, sol_hbm), (res, res_turned, res_hbm)):
+            turned[x] = jnp.swapaxes(buffer[x], 0, 1)
+            copy = pltpu.make_async_copy(turned.at[x], target.at[:, x], out_sem.at[len(copies)])
+            copy.start()
+            copies.append(copy)
     for copy in copies:
         copy.wait()
 
@@ -455,13 +478,14 @@
                 vmem((1, n_narrow - 1, 2, 128), F32),
                 vmem(((BASIS + 1) * kk, 128), F32),
                 vmem((cx, cy, 8, nz), F32),
-                dma((5 + cx * cy,)),
+                dma((4 + CHUNKS * cx + cx * cy,)),
                 dma((4,)),
                 dma((4,)),
                 dma((BASIS, 2 + 2 * CHUNKS)),
                 dma((BASIS, 2 + 2 * CHUNKS)),
                 dma((3, 2)),
                 dma((3, 2)),
+                pltpu.SemaphoreType.REGULAR((2, 4)),
             ],
             compiler_params=pltpu.CompilerParams(collective_id=0, has_side_effects=True),
         )(sources, well_columns, column_active, perm_root, storage_term, inverse_blocks)
@@ -474,7 +498,9 @@
             scratch_shapes=[
                 vmem((cx, cy, kk, nz), F32),
                 vmem((cx, cy, kk, nz), F32),
-                dma((2 * cx * cy,)),
+                vmem((cx, kk, cy, nz), F32),
+                vmem((cx, kk, cy, nz), F32),
+                dma((2 * cx,)),
             ],
         )(*(pltpu.with_memory_space_constraint(value, vmem) for value in held))
 

time: 47.9 us -> 44.7 us (0.933)
  Pallas kernels: 47.1 us -> 44 us
    pallas_call x1, Pallas kernels: 3.26 us -> 1.26 us  [on_device(): pl.pallas_call(combine, out_shape=(field, field), in_specs=[pl.BlockSpec(...]
    pallas_call x1, Pallas kernels: 43.9 us -> 42.7 us  [on_device(): pl.pallas_call(functools.partial(kernel, n_wide, n_narrow), out_shape=(vm...]
where the time goes in v4:
time: 44.7 us; the launch traced here: 44.6 us
  Pallas kernels  44 us (98%)
  between operations  0.64 us (1%)
    pallas_call x1, Pallas kernels, on_device(): pl.pallas_call(functools.partial(kernel, n_wide, n_narrow), out_shape=(vm...  42.7 us
    pallas_call x1, Pallas kernels, on_device(): pl.pallas_call(combine, out_shape=(field, field), in_specs=[pl.BlockSpec(...  1.26 us

profile of v4, /device:TPU:1, one launch (start us, length us, event | category | flops | bytes accessed | tf_op | source)
XLA Modules:
  0.0 44.6 jit_solution(15059664854282065911)
XLA Ops:
  0.6 42.7 %shard_map.77 = (f32[16,128]{1,0:T(8,128)S(1)}, f32[2,8,16,256]{3,2,1,0:T(8,128)S(1)}, f32[3,2,8,16,256]{4,3,2,1,0:T(8,128)S(1)}, f32[3,2,8,16,256]{4,3,2,1,0:T(8,128)S(1)}) custom-call(f32[16,2,8,256]{3,2,1,0:T(8,128)} %src_hbm.1, s32[16]{0:T(128)} %wells_hbm.1, s32[2,8]{1,0:T(2,128)} %active_hbm.1, f32[2,8,256]{2,1,0:T(8,128)} %perm_hbm.1, ...), custom_call_target="tpu_custom_call" | custom-call | tf_op jit(solution)/shard_map/pallas_call | solution.py:448
  43.4 1.3 %shard_map.78 = (f32[16,2,8,256]{3,2,1,0:T(8,128)}, f32[16,2,8,256]{3,2,1,0:T(8,128)}) custom-call(f32[16,128]{1,0:T(8,128)S(1)} %get-tuple-element.6.weights, f32[2,8,16,256]{3,2,1,0:T(8,128)S(1)} %get-tuple-element.7.rhs, f32[3,2,8,16,256]{4,3,2,1,0:T(8,128)S(1)} %get-tuple-element.8.zs, f32[3,2,8,16,256]{4,3,2,1,0:T(8,128)S(1)} %get-tuple-element.9.ws), custom_call_target="tpu_custom_call" | custom-call | tf_op jit(solution)/shard_map/pallas_call | solution.py:493

commit v5 on v4

--- a/solution.py
+++ b/solution.py
@@ -19,10 +19,6 @@
 
 def dot_nt(left, right, precision=EXACT):
     return lax.dot_general(left, right, (((1,), (1,)), ((), ())), precision=precision, preferred_element_type=F32)
-
-
-def dot_nn(left, right):
-    return lax.dot_general(left, right, (((1,), (0,)), ((), ())), precision=SPLIT, preferred_element_type=F32)
 
 
 def kernel(
@@ -36,8 +32,7 @@
     inv_hbm,
     weights,
     rhs,
-    zs,
-    ws,
+    split,
     wells,
     active,
     perm,
@@ -48,12 +43,18 @@
     coef_x,
     coef_pad,
     diag,
+    zs,
+    ws,
     halo_x,
     halo_y,
     part,
     wide_in,
     plane,
     plane_in,
+    part_b,
+    wide_in_b,
+    plane_b,
+    plane_in_b,
     part_c,
     wide_in_c,
     plane_c,
@@ -267,9 +268,8 @@
                     w += pair * (v - outer[ks])
                 ws[i, x, y, ks] = w
 
-    def gram(lefts, rights):
-        acc = None
-        for x, y in columns:
+    def gram(lefts, rights, cells, acc=None):
+        for x, y in cells:
             left_rows = jnp.concatenate([ref[x, y] for ref in lefts], axis=0)
             right_rows = jnp.concatenate([ref[x, y] for ref in rights], axis=0)
             product = dot_nt(left_rows, right_rows, SPLIT)
@@ -299,22 +299,25 @@
             lines = [a + b for a, b in zip(lines[::2], lines[1::2])] + lines[len(lines) // 2 * 2 :]
         return lines[0]
 
-    sums = [(part, wide_in, plane, plane_in), (part, wide_in, plane, plane_in), (part_c, wide_in_c, plane_c, plane_in_c)]
-    slot = [0, 1, 0]
+    sums = [
+        (part, wide_in, plane, plane_in),
+        (part_b, wide_in_b, plane_b, plane_in_b),
+        (part_c, wide_in_c, plane_c, plane_in_c),
+    ]
 
     def sum_wide(j, value):
-        own, into = sums[j][0].at[slot[j]], sums[j][1].at[slot[j]]
+        own, into = sums[j][0], sums[j][1]
         own[...] = value
         send_all("wide", me_w, n_wide, own, into, sum_send.at[j, 0], sum_recv.at[j, 0])
 
     def sum_narrow(j):
-        own, into, mid, last = (ref.at[slot[j]] for ref in sums[j])
+        own, into, mid, last = sums[j]
         received("wide", right, into, sum_send.at[j, 0], sum_recv.at[j, 0])
         mid[...] = add_all(own[...], into)
         send_all("narrow", me_n, n_narrow, mid, last, sum_send.at[j, 1], sum_recv.at[j, 1])
 
     def sum_done(j):
-        mid, last = sums[j][2].at[slot[j]], sums[j][3].at[slot[j]]
+        mid, last = sums[j][2], sums[j][3]
         received("narrow", above, last, sum_send.at[j, 1], sum_recv.at[j, 1])
         return add_all(mid[...], last)
 
@@ -349,24 +352,31 @@
             hear("wide", 1)
             tell("wide", 2)
         if i == 1:
-            first = gram([rhs, w_refs[0]], [z_refs[0], z_refs[1]])
+            first = gram([rhs, w_refs[0]], [z_refs[0], z_refs[1]], columns)
             hear("wide", 3)
             sum_wide(0, halve(jnp.concatenate([first[:kk], first[kk:]], axis=1)))
         if i == 2:
-            second = gram([rhs, w_refs[0], w_refs[1]], [z_refs[1], z_refs[2]])
-            line = [second[:kk, kk:], second[kk : 2 * kk, kk:], second[2 * kk :]]
-            sum_wide(1, halve(jnp.concatenate(line, axis=1)))
+            second = gram([w_refs[1]], [z_refs[1], z_refs[2]], columns)
+            sum_wide(1, jnp.concatenate([second[at : at + 4] for at in range(0, kk, 4)], axis=1))
             hear("narrow", 2)
             sum_narrow(0)
+    third = None
     for c in order:
         absorb(BASIS - 1, c)
+        third = gram([w_refs[2]], [z_refs[2]], chunk(c), third)
 
     lanes = lax.broadcasted_iota(jnp.int32, (kk, 128), 1)
     rows = lax.broadcasted_iota(jnp.int32, (kk, 128), 0)
     diagonal = lanes // kk == lax.rem(rows, 8)
-    third = gram([w_refs[2]], [z_refs[2]])
     third = jnp.where(diagonal, jnp.concatenate([third] * 8, axis=1), 0.0)
     sum_wide(2, jnp.concatenate([jnp.sum(third[:8], axis=0, keepdims=True), jnp.sum(third[8:], axis=0, keepdims=True)], axis=0))
+
+    for x, yy in columns:
+        for at, field in enumerate((zs, ws)):
+            value = jnp.concatenate([field[i, x, yy] for i in range(BASIS)], axis=0)
+            high = value.astype(jnp.bfloat16)
+            split[at, x, yy, : BASIS * kk] = high
+            split[at, x, yy, BASIS * kk :] = (value - high.astype(F32)).astype(jnp.bfloat16)
 
     matrix[...] = jnp.zeros_like(matrix)
     sum_narrow(1)
@@ -375,12 +385,14 @@
         matrix[8 * h : 8 * h + 8, 0 : 2 * kk] = first[:, 64 * h : 64 * h + 2 * kk]
         matrix[kk + 8 * h : kk + 8 * h + 8, 0 : 2 * kk] = first[:, 64 * h + 2 * kk : 64 * h + 4 * kk]
     sum_narrow(2)
+    for h in range(2):
+        piece = first[:, 64 * h + 3 * kk : 64 * h + 4 * kk]
+        matrix[8 * h : 8 * h + 8, 2 * kk : 3 * kk] = piece * BASIS_SCALE
     second = sum_done(1)
-    for h in range(2):
-        for r in range(2):
-            piece = second[:, 64 * h + r * kk : 64 * h + (r + 1) * kk]
-            matrix[r * kk + 8 * h : r * kk + 8 * h + 8, 2 * kk : 3 * kk] = piece
-        matrix[2 * kk + 8 * h : 2 * kk + 8 * h + 8, kk : 3 * kk] = second[:, 64 * h + 2 * kk : 64 * h + 4 * kk]
+    for g in range(4):
+        piece = second[:, 2 * kk * g : 2 * kk * (g + 1)]
+        matrix[2 * kk + 4 * g : 2 * kk + 4 * g + 4, kk : 3 * kk] = piece
+        matrix[kk + 4 * g : kk + 4 * g + 4, 2 * kk : 3 * kk] = piece[:, :kk]
     pick_rows = lax.broadcasted_iota(jnp.int32, (2 * kk, 128), 0)
     pick_lanes = lax.broadcasted_iota(jnp.int32, (2 * kk, 128), 1)
     pick = jnp.where(pick_lanes == pick_rows + kk, 1.0, 0.0)
@@ -418,16 +430,26 @@
     weights[...] = system[:kk]
 
 
-def combine(weights, rhs, zs, ws, sol_hbm, res_hbm, sol, res, sol_turned, res_turned, out_sem):
+def combine(weights, rhs, split, sol_hbm, res_hbm, sol, res, sol_turned, res_turned, out_sem):
     cx, cy, kk, nz = rhs.shape
     y = weights[:, : BASIS * kk]
+    high = y.astype(jnp.bfloat16)
+    low = (y - high.astype(F32)).astype(jnp.bfloat16)
+    factors = jnp.concatenate(
+        [jnp.concatenate([high, high], axis=1), jnp.concatenate([low, jnp.zeros_like(low)], axis=1)], axis=0
+    )
+
+    def weighted(at, x, yy):
+        out = lax.dot_general(
+            factors, split[at, x, yy], (((1,), (0,)), ((), ())), preferred_element_type=F32
+        )
+        return out[:kk] + out[kk:]
+
     copies = []
     for x in range(cx):
         for yy in range(cy):
-            basis = jnp.concatenate([zs[i, x, yy] for i in range(BASIS)], axis=0)
-            image = jnp.concatenate([ws[i, x, yy] for i in range(BASIS)], axis=0)
-            sol[x, yy] = dot_nn(y, basis)
-            res[x, yy] = rhs[x, yy] - dot_nn(y, image)
+            sol[x, yy] = weighted(0, x, yy)
+            res[x, yy] = rhs[x, yy] - weighted(1, x, yy)
         for buffer, turned, target in ((sol, sol_turned, sol_hbm), (res, res_turned, res_hbm)):
             turned[x] = jnp.swapaxes(buffer[x], 0, 1)
             copy = pltpu.make_async_copy(turned.at[x], target.at[:, x], out_sem.at[len(copies)])
@@ -450,11 +472,10 @@
             out_shape=(
                 vmem((kk, 128), F32),
                 vmem((cx, cy, kk, nz), F32),
-                vmem((BASIS, cx, cy, kk, nz), F32),
-                vmem((BASIS, cx, cy, kk, nz), F32),
+                vmem((2, cx, cy, 2 * BASIS * kk, nz), jnp.bfloat16),
             ),
             in_specs=[pl.BlockSpec(memory_space=pl.ANY)] * 6,
-            out_specs=(pl.BlockSpec(memory_space=vmem),) * 4,
+            out_specs=(pl.BlockSpec(memory_space=vmem),) * 3,
             scratch_shapes=[
                 pltpu.SMEM(well_columns.shape, jnp.int32),
                 pltpu.SMEM(column_active.shape, jnp.int32),
@@ -466,16 +487,20 @@
                 vmem((2, cy, nz), F32),
                 vmem((cx + 2, cy + 2, 8, nz), F32),
                 vmem((cx, cy, nz), F32),
+                vmem((BASIS, cx, cy, kk, nz), F32),
+                vmem((BASIS, cx, cy, kk, nz), F32),
                 vmem((BASIS, 2, cy, kk, nz), F32),
                 vmem((BASIS, 2, cx, kk, nz), F32),
-                vmem((2, 8, 128), F32),
-                vmem((2, n_wide - 1, 8, 128), F32),
-                vmem((2, 8, 128), F32),
-                vmem((2, n_narrow - 1, 8, 128), F32),
-                vmem((1, 2, 128), F32),
-                vmem((1, n_wide - 1, 2, 128), F32),
-                vmem((1, 2, 128), F32),
-                vmem((1, n_narrow - 1, 2, 128), F32),
+                *(
+                    vmem(shape, F32)
+                    for height in (8, 4, 2)
+                    for shape in (
+                        (height, 128),
+                        (n_wide - 1, height, 128),
+                        (height, 128),
+                        (n_narrow - 1, height, 128),
+                    )
+                ),
                 vmem(((BASIS + 1) * kk, 128), F32),
                 vmem((cx, cy, 8, nz), F32),
                 dma((4 + CHUNKS * cx + cx * cy,)),
@@ -493,7 +518,7 @@
         return pl.pallas_call(
             combine,
             out_shape=(field, field),
-            in_specs=[pl.BlockSpec(memory_space=vmem)] * 4,
+            in_specs=[pl.BlockSpec(memory_space=vmem)] * 3,
             out_specs=(pl.BlockSpec(memory_space=pl.ANY),) * 2,
             scratch_shapes=[
                 vmem((cx, cy, kk, nz), F32),

time: 44.7 us -> 44 us (0.984)
  Pallas kernels: 44 us -> 43.2 us
    pallas_call x1, Pallas kernels: 42.7 us -> 42 us  [on_device(): pl.pallas_call(functools.partial(kernel, n_wide, n_narrow), out_shape=(vm...]
where the time goes in v5:
time: 44 us; the launch traced here: 43.8 us
  Pallas kernels  43.2 us (98%)
  between operations  0.64 us (1%)
    pallas_call x1, Pallas kernels, on_device(): pl.pallas_call(functools.partial(kernel, n_wide, n_narrow), out_shape=(vm...  42 us
    pallas_call x1, Pallas kernels, on_device(): pl.pallas_call(combine, out_shape=(field, field), in_specs=[pl.BlockSpec(...  1.17 us

profile of v5, /device:TPU:1, one launch (start us, length us, event | category | flops | bytes accessed | tf_op | source)
XLA Modules:
  0.0 43.8 jit_solution(7915217884478793126)
XLA Ops:
  0.6 42.0 %shard_map.77 = (f32[16,128]{1,0:T(8,128)S(1)}, f32[2,8,16,256]{3,2,1,0:T(8,128)S(1)}, bf16[2,2,8,96,256]{4,3,2,1,0:T(8,128)(2,1)S(1)}) custom-call(f32[16,2,8,256]{3,2,1,0:T(8,128)} %src_hbm.1, s32[16]{0:T(128)} %wells_hbm.1, s32[2,8]{1,0:T(2,128)} %active_hbm.1, f32[2,8,256]{2,1,0:T(8,128)} %perm_hbm.1, f32[2,8,256]{2,1,0:T(8,128)} %storage_hbm.1, ...), custom_call_target="tpu_custom_call" | custom-call | tf_op jit(solution)/shard_map/pallas_call | solution.py:470
  42.7 1.2 %shard_map.78 = (f32[16,2,8,256]{3,2,1,0:T(8,128)}, f32[16,2,8,256]{3,2,1,0:T(8,128)}) custom-call(f32[16,128]{1,0:T(8,128)S(1)} %get-tuple-element.5.weights, f32[2,8,16,256]{3,2,1,0:T(8,128)S(1)} %get-tuple-element.6.rhs, bf16[2,2,8,96,256]{4,3,2,1,0:T(8,128)(2,1)S(1)} %get-tuple-element.7.split), custom_call_target="tpu_custom_call" | custom-call | tf_op jit(solution)/shard_map/pallas_call | solution.py:518

commit v6 on v5

--- a/solution.py
+++ b/solution.py
@@ -338,6 +338,9 @@
             tell("wide", 3)
             hear("narrow", 1)
             tell("narrow", 2)
+        if i == 2:
+            second = gram([w_refs[1]], [z_refs[1], z_refs[2]], columns)
+            sum_wide(1, jnp.concatenate([second[at : at + 4] for at in range(0, kk, 4)], axis=1))
         operate_inside(i)
         if i == 0:
             for copy in coef_copies:
@@ -356,8 +359,6 @@
             hear("wide", 3)
             sum_wide(0, halve(jnp.concatenate([first[:kk], first[kk:]], axis=1)))
         if i == 2:
-            second = gram([w_refs[1]], [z_refs[1], z_refs[2]], columns)
-            sum_wide(1, jnp.concatenate([second[at : at + 4] for at in range(0, kk, 4)], axis=1))
             hear("narrow", 2)
             sum_narrow(0)
     third = None
@@ -367,7 +368,7 @@
 
     lanes = lax.broadcasted_iota(jnp.int32, (kk, 128), 1)
     rows = lax.broadcasted_iota(jnp.int32, (kk, 128), 0)
-    diagonal = lanes // kk == lax.rem(rows, 8)
+    diagonal = lanes // kk == lax.rem(10 - lax.rem(rows, 8), 8)
     third = jnp.where(diagonal, jnp.concatenate([third] * 8, axis=1), 0.0)
     sum_wide(2, jnp.concatenate([jnp.sum(third[:8], axis=0, keepdims=True), jnp.sum(third[8:], axis=0, keepdims=True)], axis=0))
 
@@ -419,10 +420,13 @@
         system = eliminate(system, kk + k, k)
 
     third = sum_done(2)
-    third = jnp.concatenate([jnp.broadcast_to(third[h : h + 1], (8, 128)) for h in range(2)], axis=0)
-    third = jnp.where(diagonal, third, 0.0)
-    for shift in (64, 32, 16):
-        third = third + pltpu.roll(third, shift, 1)
+    third = jnp.concatenate(
+        [
+            pltpu.roll(jnp.broadcast_to(third[h : h + 1], (8, 128)), 0, 1, stride=kk, stride_axis=0)
+            for h in range(2)
+        ],
+        axis=0,
+    )
     third = jnp.where((lanes >= 2 * kk) & (lanes < 3 * kk), third, 0.0)
     system = jnp.concatenate([system[:kk], system[3 * kk :] + third], axis=0)
     for k in range(0, kk, 2):

time: 44 us -> 43.8 us (level)
  no operation moved by 1% of the time
where the time goes in v6:
time: 43.8 us; the launch traced here: 43.7 us
  Pallas kernels  43.1 us (98%)
  between operations  0.64 us (1%)
    pallas_call x1, Pallas kernels, on_device(): pl.pallas_call(functools.partial(kernel, n_wide, n_narrow), out_shape=(vm...  41.9 us
    pallas_call x1, Pallas kernels, on_device(): pl.pallas_call(combine, out_shape=(field, field), in_specs=[pl.BlockSpec(...  1.17 us

profile of v6, /device:TPU:1, one launch (start us, length us, event | category | flops | bytes accessed | tf_op | source)
XLA Modules:
  0.0 43.7 jit_solution(5036889802672904688)
XLA Ops:
  0.6 41.9 %shard_map.77 = (f32[16,128]{1,0:T(8,128)S(1)}, f32[2,8,16,256]{3,2,1,0:T(8,128)S(1)}, bf16[2,2,8,96,256]{4,3,2,1,0:T(8,128)(2,1)S(1)}) custom-call(f32[16,2,8,256]{3,2,1,0:T(8,128)} %src_hbm.1, s32[16]{0:T(128)} %wells_hbm.1, s32[2,8]{1,0:T(2,128)} %active_hbm.1, f32[2,8,256]{2,1,0:T(8,128)} %perm_hbm.1, f32[2,8,256]{2,1,0:T(8,128)} %storage_hbm.1, ...), custom_call_target="tpu_custom_call" | custom-call | tf_op jit(solution)/shard_map/pallas_call | solution.py:474
  42.5 1.2 %shard_map.78 = (f32[16,2,8,256]{3,2,1,0:T(8,128)}, f32[16,2,8,256]{3,2,1,0:T(8,128)}) custom-call(f32[16,128]{1,0:T(8,128)S(1)} %get-tuple-element.5.weights, f32[2,8,16,256]{3,2,1,0:T(8,128)S(1)} %get-tuple-element.6.rhs, bf16[2,2,8,96,256]{4,3,2,1,0:T(8,128)(2,1)S(1)} %get-tuple-element.7.split), custom_call_target="tpu_custom_call" | custom-call | tf_op jit(solution)/shard_map/pallas_call | solution.py:522
